TPU v7x, 256 devices: a whole 4x4x8 slice. The times are simulated.
256 devices in a mesh: head: 4 (over x), blk: 64 (over y, z, core).
Axes of the slice: x: 4, y: 4, z: 8, core: 2. Of those that a mesh axis runs over, the one named last changes fastest.
Arguments:
- doc_x: bfloat16 [65536, 1024], P('blk'), may hold values from -6 to 6
- doc_seg: int32 [65536], P('blk'), may hold values from 0 to 1023, as said below
- doc_query: int32 [1024], replicated, may hold values from 0 to 7
- doc_var: int32 [65536], P('blk'), may hold values from 0 to 7
- query_len: int32 [8], replicated, may hold values from 256 to 4096, as said below
- block_perm: int32 [64], replicated, may hold values from 0 to 63, each once
- cache_k: bfloat16 [32768, 1024], P('blk', 'head'), may hold values from -164 to 164
- cache_v: bfloat16 [32768, 1024], P('blk', 'head'), may hold values from -6 to 6
- cache_var: int32 [32768], P('blk'), may hold values from 0 to 7
- w_query: bfloat16 [1024, 1024], P(None, 'head'), may hold values from -0.1875 to 0.1875
- w_key: bfloat16 [1024, 1024], P(None, 'head'), may hold values from -0.5 to 0.5
- w_value: bfloat16 [1024, 1024], P(None, 'head'), may hold values from -0.1875 to 0.1875
- w_out: bfloat16 [1024, 1024], P('head'), may hold values from -0.1875 to 0.1875
- var_bias: float32 [2, 16], P(None, 'head'), may hold values from -1 to 1
- norm_gain: float32 [1024], replicated, may hold values from 0.1 to 1.9
- readout: float32 [1024], replicated, may hold values from -1.5 to 1.5
Outputs:
- update: float32 [65536, 1024], P('blk', 'head')
- pooled: float32 [1024], P('blk')
Inputs may be any that keep to these rules, and one draw needn't show every extreme that they name: `doc_seg`: index i of blk holds documents i * 16 to (i + 1) * 16 - 1 whole; its 1024 tokens form 8 runs of 128 tokens, run j holding its documents 2j and 2j + 1, both of one query, and the 8 runs of one index belong to 8 different queries. query_len[0] = 4096.
All inputs are finite; a program needn't handle non-finite values.
Results may differ from a plain program's by a relative error of at most 0.012.
The roundings to bfloat16 on the way count: a program that leaves them out, or rounds other values in their place, can miss the bound.
Values may be sent and summed in bfloat16 or wider, within the bound.
A program may use at most 128 MiB of HBM per device.

v0:
```python
import jax
import jax.numpy as jnp
from jax import lax
from jax.sharding import PartitionSpec as P

D = 1024
DH = 64
QUERIES = 8


def rotary(projected, positions):
    row_count = projected.shape[0]
    head_count = projected.shape[1] // DH
    half_size = DH // 2
    shaped = projected.reshape(row_count, head_count, DH)
    frequency = 10000.0 ** (-jnp.arange(half_size, dtype=jnp.float32) / half_size)
    angles = positions.astype(jnp.float32)[:, None] * frequency[None, :]
    cosine = jnp.cos(angles)[:, None, :]
    sine_part = jnp.sin(angles)[:, None, :]
    first_half = shaped[:, :, :half_size]
    second_half = shaped[:, :, half_size:]
    turned = jnp.concatenate(
        [
            first_half * cosine - second_half * sine_part,
            second_half * cosine + first_half * sine_part,
        ],
        axis=2,
    )
    return turned.reshape(row_count, head_count * DH)


def softmax_part(scores, allowed):
    scores = jnp.where(allowed, scores, -1e30)
    peak = jnp.max(scores, axis=-1)
    weights = jnp.where(allowed, jnp.exp(scores - peak[..., None]), 0.0)
    return (peak, jnp.sum(weights, axis=-1), weights.astype(jnp.bfloat16))


def cache_part(
    recv_q, recv_var, cache_keys, cache_values, cache_var, row_valid, bias_same, bias_other
):
    source_count = recv_q.shape[0]
    item_count = recv_q.shape[1]
    col_count = recv_q.shape[2]
    head_count = cache_keys.shape[1]
    total_rows = source_count * item_count
    block_rows = 512
    block_count = total_rows // block_rows
    flat_q = recv_q.reshape(block_count, block_rows, head_count, DH)
    flat_var = recv_var.reshape(block_count, block_rows).astype(jnp.int32)

    def one_block(block_inputs):
        block_q, block_var = block_inputs
        scores = (
            jnp.einsum("thd,rhd->htr", block_q, cache_keys, preferred_element_type=jnp.float32)
            * 0.125
        )
        scores = scores + jnp.where(
            (block_var[:, None] == cache_var[None, :])[None], bias_same, bias_other
        )
        allowed = jnp.broadcast_to(row_valid[None, None, :], scores.shape)
        peak, total_weight, weights = softmax_part(scores, allowed)
        mixed = jnp.einsum(
            "htr,rhd->thd", weights, cache_values, preferred_element_type=jnp.float32
        )
        return (peak.T, total_weight.T, mixed.reshape(block_rows, col_count))

    maxima, totals, sums = lax.map(one_block, (flat_q, flat_var))
    return (
        maxima.reshape(source_count, item_count, head_count),
        totals.reshape(source_count, item_count, head_count),
        sums.reshape(source_count, item_count, col_count),
    )


def body(
    doc_x,
    doc_seg,
    doc_query,
    doc_var,
    query_len,
    block_perm,
    cache_k,
    cache_v,
    cache_var,
    w_query,
    w_key,
    w_value,
    w_out,
    var_bias,
    norm_gain,
    readout,
):
    row_count = doc_x.shape[0]
    col_count = w_query.shape[1]
    head_count = col_count // DH
    cache_count = cache_k.shape[0]
    blk_count = lax.axis_size("blk")
    blk_index = lax.axis_index("blk")
    head_index = lax.axis_index("head")
    blocks_each = blk_count // QUERIES
    slot_count = QUERIES
    slot_rows = row_count // slot_count
    doc_count = 2 * slot_count
    first_doc = blk_index * doc_count
    local_seg = doc_seg - first_doc
    member = (local_seg[:, None] == jnp.arange(doc_count, dtype=jnp.int32)[None, :]).astype(
        jnp.int32
    )
    lengths = jnp.sum(member, axis=0)
    starts = jnp.cumsum(lengths) - lengths
    first_pos = jnp.dot(member, starts)
    own_docs_query = lax.dynamic_slice_in_dim(doc_query, first_doc, doc_count)
    query_table = (own_docs_query[:, None] == jnp.arange(QUERIES, dtype=jnp.int32)[None, :]).astype(
        jnp.int32
    )
    doc_len = jnp.sum(query_table * query_len[None, :], axis=1)
    tok_len = jnp.dot(member, doc_len)
    positions = tok_len + jnp.arange(row_count, dtype=jnp.int32) - first_pos
    query_rot = rotary(
        jnp.dot(doc_x, w_query, preferred_element_type=jnp.float32), positions
    ).astype(jnp.bfloat16)
    key_rot = rotary(jnp.dot(doc_x, w_key, preferred_element_type=jnp.float32), positions).astype(
        jnp.bfloat16
    )
    value_proj = jnp.dot(doc_x, w_value, preferred_element_type=jnp.float32).astype(jnp.bfloat16)
    bias_same = var_bias[0][:, None, None]
    bias_other = var_bias[1][:, None, None]
    shaped_q = query_rot.reshape(slot_count, slot_rows, head_count, DH)
    shaped_k = key_rot.reshape(slot_count, slot_rows, head_count, DH)
    shaped_v = value_proj.reshape(slot_count, slot_rows, head_count, DH)
    slot_seg = local_seg.reshape(slot_count, slot_rows)
    slot_var = doc_var.reshape(slot_count, slot_rows)
    self_scores = (
        jnp.einsum("gthd,gshd->ghts", shaped_q, shaped_k, preferred_element_type=jnp.float32)
        * 0.125
    )
    self_scores = self_scores + jnp.where(
        (slot_var[:, :, None] == slot_var[:, None, :])[:, None], bias_same[None], bias_other[None]
    )
    self_allowed = (slot_seg[:, :, None] == slot_seg[:, None, :])[:, None]
    self_peak, self_total, self_weights = softmax_part(self_scores, self_allowed)
    self_sum = jnp.einsum(
        "ghts,gshd->gthd", self_weights, shaped_v, preferred_element_type=jnp.float32
    )
    self_peak = self_peak.transpose(0, 2, 1)
    self_total = self_total.transpose(0, 2, 1)
    slot_query = own_docs_query.reshape(slot_count, 2)[:, 0]
    block_query = block_perm // blocks_each
    slot_match = block_query[:, None] == slot_query[None, :]
    slot_pick = jnp.sum(
        slot_match.astype(jnp.int32) * jnp.arange(slot_count, dtype=jnp.int32)[None, :], axis=1
    )
    send_q = jnp.take(query_rot.reshape(slot_count, slot_rows, col_count), slot_pick, axis=0)
    send_var = jnp.take(slot_var, slot_pick, axis=0).astype(jnp.bfloat16)
    my_block = lax.dynamic_slice_in_dim(block_perm, blk_index, 1)[0]
    my_query = my_block // blocks_each
    first_row = my_block % blocks_each * cache_count
    my_len = lax.dynamic_slice_in_dim(query_len, my_query, 1)[0]
    row_valid = first_row + jnp.arange(cache_count, dtype=jnp.int32) < my_len
    cache_keys = cache_k.reshape(cache_count, head_count, DH)
    cache_values = cache_v.reshape(cache_count, head_count, DH)
    recv_q, recv_var = (
        lax.all_to_all(send_q, "blk", split_axis=0, concat_axis=0, tiled=True),
        lax.all_to_all(send_var, "blk", split_axis=0, concat_axis=0, tiled=True),
    )
    maxima, totals, sums = cache_part(
        recv_q, recv_var, cache_keys, cache_values, cache_var, row_valid, bias_same, bias_other
    )
    got_max, got_total, got_sum = (
        lax.all_to_all(maxima, "blk", split_axis=0, concat_axis=0, tiled=True),
        lax.all_to_all(totals, "blk", split_axis=0, concat_axis=0, tiled=True),
        lax.all_to_all(sums, "blk", split_axis=0, concat_axis=0, tiled=True),
    )
    match_float = slot_match.astype(jnp.float32)
    spread_max = jnp.where(slot_match[:, :, None, None], got_max[:, None], -1e30)
    cache_peak = jnp.max(spread_max, axis=0)
    peak = jnp.maximum(cache_peak, self_peak)
    device_peak = jnp.take(peak, slot_pick, axis=0)
    factor = jnp.exp(got_max - device_peak)
    cache_total = jnp.einsum(
        "dg,dth->gth", match_float, got_total * factor, precision=lax.Precision.HIGHEST
    )
    scaled_sum = got_sum.reshape(blk_count, slot_rows, head_count, DH) * factor[..., None]
    cache_sum = jnp.einsum(
        "dg,dthe->gthe", match_float, scaled_sum, precision=lax.Precision.HIGHEST
    )
    self_factor = jnp.exp(self_peak - peak)
    numerator = cache_sum + self_sum * self_factor[..., None]
    denominator = cache_total + self_total * self_factor
    attended = (
        (numerator / denominator[..., None]).reshape(row_count, col_count).astype(jnp.bfloat16)
    )
    partial_update = jnp.dot(attended, w_out, preferred_element_type=jnp.float32)
    x_float = doc_x.astype(jnp.float32)
    whole_sum = lax.psum(partial_update, "head")
    hidden = x_float + whole_sum
    square_sum = jnp.sum(hidden * hidden, axis=1)
    weighted = jnp.sum(hidden * norm_gain * readout, axis=1)
    update = lax.dynamic_slice_in_dim(whole_sum, head_index * col_count, col_count, 1)
    token_score = weighted * lax.rsqrt(square_sum / D + 1e-06)
    pooled_sum = jnp.dot(token_score, member.astype(jnp.float32), precision=lax.Precision.HIGHEST)
    return (update, pooled_sum / lengths.astype(jnp.float32))


def solution(mesh):
    return jax.shard_map(
        body,
        mesh=mesh,
        in_specs=(
            P("blk", None),
            P("blk"),
            P(),
            P("blk"),
            P(),
            P(),
            P("blk", "head"),
            P("blk", "head"),
            P("blk"),
            P(None, "head"),
            P(None, "head"),
            P(None, "head"),
            P("head", None),
            P(None, "head"),
            P(),
            P(),
        ),
        out_specs=(P("blk", "head"), P("blk")),
        check_vma=False,
    )
```

profile of v0, /device:TPU:8, one launch (start us, length us, event | category | flops | bytes accessed | tf_op | source)
XLA Modules:
  0.0 645.8 jit_solution(2000789111802115484)
XLA Ops:
  11.0 12.1 %all-to-all-start.1 = ((bf16[64,1,128]{2,1,0:T(2,128)(2,1)}), bf16[64,1,128]{2,1,0:T(2,128)(2,1)S(1)}, u32[]{:S(2)}, u32[]{:S(2)}) async-start(bf16[64,1,128]{2,1,0:T(2,128)(2,1)} %copy.100), calls=%async_computation.1 | async-start | bytes 65536 | tf_op jit(solution)/shard_map/all_to_all | solution.py:165
  29.0 2.8 gather_fusion
  31.8 4.6 broadcast_select_fusion
  36.4 10.7 %all-to-all-start = ((bf16[64,128,256]{2,1,0:T(8,128)(2,1)}), bf16[64,128,256]{2,1,0:T(8,128)(2,1)}, u32[]{:S(2)}, u32[]{:S(2)}) async-start(bf16[64,128,256]{2,1,0:T(8,128)(2,1)} %broadcast_select_fusion), calls=%async_computation | async-start | bytes 8388608 | tf_op jit(solution)/shard_map/all_to_all | solution.py:164
  52.0 89.9 %all-to-all-done = bf16[64,128,256]{2,1,0:T(8,128)(2,1)} async-done(((bf16[64,128,256]{2,1,0:T(8,128)(2,1)}), bf16[64,128,256]{2,1,0:T(8,128)(2,1)}, u32[]{:S(2)}, u32[]{:S(2)}) %all-to-all-start) | async-done | bytes 4194336 | tf_op jit(solution)/shard_map/all_to_all | solution.py:164
  141.9 12.9 %reshape.307 = bf16[16,512,4,64]{3,2,1,0:T(4,128)(2,1)} reshape(bf16[64,128,256]{2,1,0:T(8,128)(2,1)} %all-to-all-done) | data formatting | bytes 8388608 | tf_op jit(solution)/shard_map/reshape | solution.py:49
  154.8 12.7 %copy.102 = bf16[16,512,4,64]{1,3,2,0:T(8,128)(2,1)} copy(bf16[16,512,4,64]{3,2,1,0:T(4,128)(2,1)} %reshape.307) | data formatting | bytes 8388608
  167.5 122.0 %while.15 = (s32[]{:T(128)}, f32[16,512,4]{1,2,0:T(4,128)S(1)}, f32[16,512,4]{1,2,0:T(4,128)S(1)}, f32[16,512,256]{2,1,0:T(8,128)}, bf16[16,512,4,64]{1,3,2,0:T(...) while((s32[]{:T(128)}, f32[16,512,4]{1,2,0:T(4,128)S(1)}, ...), condition=%wide.region_7.8_spmd.clone, body=%wide.region_4.7_spmd.clone.sunk | while | flops 288617472 | bytes 17115396 | solution.py:68
  168.5 2.5 fusion.87
  176.1 2.5 fusion.87
  183.8 2.5 fusion.87
  191.4 2.5 fusion.87
  199.0 2.5 fusion.87
  206.6 2.5 fusion.87
  214.2 2.5 fusion.87
  229.5 2.5 fusion.87
  244.7 2.5 fusion.87
  252.3 2.5 fusion.87
  259.9 2.5 fusion.87
  275.2 2.5 fusion.87
  289.5 16.1 %all_to_all.26 = f32[64,128,4]{1,2,0:T(4,128)} all-to-all(f32[64,128,4]{1,2,0:T(4,128)S(1)} %bitcast.155), channel_id=1, replica_groups=mesh['head'=4,'blk'=64] {'blk'}, dimensions={0} | all-to-all | bytes 262144 | tf_op jit(solution)/shard_map/all_to_all | solution.py:172
  305.6 15.0 %all_to_all.27 = f32[64,128,4]{1,2,0:T(4,128)S(1)} all-to-all(f32[64,128,4]{1,2,0:T(4,128)S(1)} %bitcast.154), channel_id=1, replica_groups=mesh['head'=4,'blk'=64] {'blk'}, dimensions={0} | all-to-all | bytes 262144 | tf_op jit(solution)/shard_map/all_to_all | solution.py:171
  320.6 6.7 %all-to-all-start.2 = ((f32[64,128,256]{2,1,0:T(8,128)}), f32[64,128,256]{2,1,0:T(8,128)}, u32[]{:S(2)}, u32[]{:S(2)}) async-start(f32[64,128,256]{2,1,0:T(8,128)} %bitcast.145), calls=%async_computation.2 | async-start | bytes 16777216 | tf_op jit(solution)/shard_map/all_to_all | solution.py:173
  329.0 2.5 convolution_convert_fusion
  331.6 2.8 reshape.308
  341.2 170.5 %all-to-all-done.2 = f32[64,128,256]{2,1,0:T(8,128)} async-done(((f32[64,128,256]{2,1,0:T(8,128)}), f32[64,128,256]{2,1,0:T(8,128)}, u32[]{:S(2)}, u32[]{:S(2)}) %all-to-all-start.2) | async-done | bytes 8388640 | tf_op jit(solution)/shard_map/all_to_all | solution.py:173
  511.7 9.0 %copy.104 = f32[64,128,256]{1,2,0:T(8,128)} copy(f32[64,128,256]{2,1,0:T(8,128)} %all-to-all-done.2) | data formatting | bytes 16777216 | tf_op jit(solution)/shard_map/all_to_all | solution.py:173
  520.6 4.6 broadcast_multiply_fusion
  525.3 8.5 %fusion.24 = bf16[8,128,4,64]{1,0,3,2:T(8,128)(2,1)S(1)} fusion(f32[64,128,4,64]{1,3,2,0:T(8,128)S(1)} %broadcast_multiply_fusion, f32[8,4,64,128]{3,2,1,0:T(8,128)S(1)} %copy-done.3, f32[8,128,4]{1,0,2:T(8,128)S(1)} %convolution_add_fusion, f32[8,128,4]{1,0,2:T(8,128)S(1)} %get-tuple-element.189, s32[64]{0:T(128)S(1)} %copy-done.16, s32[8]{0:T(128)S(1)} %copy-done.13), kind=kOutput, calls=%fused_computation.36 | convolution fusion | flops 202375680 | bytes 9994528 | tf_op jit(solution)/shard_map/dg,dthe->gthe/dot_general | solution.py:185
  533.8 2.7 fusion.34
  536.6 96.1 %all-reduce.2.cloned.1.call-done = f32[1024,1024]{1,0:T(8,128)} async-done(((f32[1024,1024]{1,0:T(8,128)}), f32[1024,1024]{1,0:T(8,128)}) %all-reduce.2.cloned.1.call-update) | async-done | bytes 4194320 | tf_op jit(solution)/shard_map/psum | solution.py:196
  632.7 3.3 multiply_reduce_fusion
  (247 shorter events, 115.1 us)
Async XLA Ops:
  7.2 526.6 %copy-start = (bf16[256,1024]{1,0:T(8,128)(2,1)S(1)}, bf16[256,1024]{1,0:T(8,128)(2,1)}, u32[]{:S(2)}) copy-start(bf16[256,1024]{1,0:T(8,128)(2,1)} %param.30) | copy-start | bytes 1572868
  7.9 319.7 %copy-start.15 = (s32[64]{0:T(128)}, s32[64]{0:T(128)S(1)}, u32[]{:S(2)}) copy-start(s32[64]{0:T(128)S(1)} %and_select_fusion) | copy-start | bytes 772
  8.9 318.7 %copy-start.12 = (s32[8]{0:T(128)}, s32[8]{0:T(128)S(1)}, u32[]{:S(2)}) copy-start(s32[8]{0:T(128)S(1)} %slice_reduce_fusion) | copy-start | bytes 100
  9.0 22.8 %copy-start.17 = (pred[64]{0:T(512)(128)(4,1)}, pred[64]{0:T(512)(128)(4,1)S(1)}, u32[]{:S(2)}) copy-start(pred[64]{0:T(512)(128)(4,1)S(1)} %compare_and_fusion) | copy-start | bytes 196
  9.0 20.0 %copy-start.14 = (s32[1024]{0:T(1024)}, s32[1024]{0:T(1024)S(1)}, u32[]{:S(2)}) copy-start(s32[1024]{0:T(1024)S(1)} %pad_clamp_fusion) | copy-start | bytes 12292
  11.0 25.4 %all-to-all-start.1 = ((bf16[64,1,128]{2,1,0:T(2,128)(2,1)}), bf16[64,1,128]{2,1,0:T(2,128)(2,1)S(1)}, u32[]{:S(2)}, u32[]{:S(2)}) async-start(bf16[64,1,128]{2,1,0:T(2,128)(2,1)} %copy.100), calls=%async_computation.1 | async-start | bytes 65536 | tf_op jit(solution)/shard_map/all_to_all | solution.py:165
  23.8 4.8 copy-start.10
  24.0 0.5 copy-start.21
  36.4 10.7 %copy-start.26 = (s32[64]{0:T(128)S(1)}, s32[64]{0:T(128)}, u32[]{:S(2)}) copy-start(s32[64]{0:T(128)} %param.23) | copy-start | bytes 772
  36.4 13.9 %copy-start.6 = (bf16[512,256]{1,0:T(8,128)(2,1)S(1)}, bf16[512,256]{1,0:T(8,128)(2,1)}, u32[]{:S(2)}) copy-start(bf16[512,256]{1,0:T(8,128)(2,1)} %param.24) | copy-start | bytes 786436
  36.4 14.1 %copy-start.7 = (bf16[512,256]{1,0:T(8,128)(2,1)S(1)}, bf16[512,256]{1,0:T(8,128)(2,1)}, u32[]{:S(2)}) copy-start(bf16[512,256]{1,0:T(8,128)(2,1)} %param.25) | copy-start | bytes 786436
  36.4 14.3 %copy-start.27 = (s32[8]{0:T(128)S(1)}, s32[8]{0:T(128)}, u32[]{:S(2)}) copy-start(s32[8]{0:T(128)} %param.22) | copy-start | bytes 100
  36.4 14.9 %copy-start.23 = (f32[2,4]{1,0:T(2,128)S(1)}, f32[2,4]{1,0:T(2,128)}, u32[]{:S(2)}) copy-start(f32[2,4]{1,0:T(2,128)} %param.31) | copy-start | bytes 100
  36.4 105.5 %all-to-all-start = ((bf16[64,128,256]{2,1,0:T(8,128)(2,1)}), bf16[64,128,256]{2,1,0:T(8,128)(2,1)}, u32[]{:S(2)}, u32[]{:S(2)}) async-start(bf16[64,128,256]{2,1,0:T(8,128)(2,1)} %broadcast_select_fusion), calls=%async_computation | async-start | bytes 8388608 | tf_op jit(solution)/shard_map/all_to_all | solution.py:164
  154.8 12.7 %copy-start.8 = (s32[512]{0:T(512)S(1)}, s32[512]{0:T(512)}, u32[]{:S(2)}) copy-start(s32[512]{0:T(512)} %param.26) | copy-start | bytes 6148
  320.6 8.4 %copy-start.1 = (bf16[1024,1024]{1,0:T(8,128)(2,1)S(1)}, bf16[1024,1024]{1,0:T(8,128)(2,1)}, u32[]{:S(2)}) copy-start(bf16[1024,1024]{1,0:T(8,128)(2,1)} %param.18) | copy-start | bytes 6291460
  320.6 191.1 %all-to-all-start.2 = ((f32[64,128,256]{2,1,0:T(8,128)}), f32[64,128,256]{2,1,0:T(8,128)}, u32[]{:S(2)}, u32[]{:S(2)}) async-start(f32[64,128,256]{2,1,0:T(8,128)} %bitcast.145), calls=%async_computation.2 | async-start | bytes 16777216 | tf_op jit(solution)/shard_map/all_to_all | solution.py:173
  327.3 7.0 %copy-start.9 = (s32[1024]{0:T(1024)S(1)}, s32[1024]{0:T(1024)}, u32[]{:S(2)}) copy-start(s32[1024]{0:T(1024)} %param.19) | copy-start | bytes 12292
  327.3 7.0 %copy-start.2 = (s32[1024]{0:T(1024)S(1)}, s32[1024]{0:T(1024)}, u32[]{:S(2)}) copy-start(s32[1024]{0:T(1024)} %param.21) | copy-start | bytes 12292
  327.3 305.4 %all-reduce.2.cloned.1.call-start = ((), (), s32[]{:S(2)}) async-start(), calls=%async_computation.5 | async-start | bytes 8388608 | tf_op jit(solution)/shard_map/psum | solution.py:196
  334.3 2.4 copy-start.24
  334.3 2.4 copy-start.25
  336.8 1.3 copy-start.4
  339.8 1.0 copy-start.5
  339.8 1.0 copy-start.18
  339.8 1.1 copy-start.13
  339.8 1.1 copy-start.16
  520.6 4.7 copy-start.3
  536.5 96.2 %copy-start.19 = (f32[1024]{0:T(1024)S(1)}, f32[1024]{0:T(1024)}, u32[]{:S(2)}) copy-start(f32[1024]{0:T(1024)} %param.33) | copy-start | bytes 12292
  536.5 96.2 %copy-start.20 = (f32[1024]{0:T(1024)S(1)}, f32[1024]{0:T(1024)}, u32[]{:S(2)}) copy-start(f32[1024]{0:T(1024)} %param.32) | copy-start | bytes 12292
  536.6 99.4 %copy-start.11 = (s32[1024]{0:T(1024)S(1)}, s32[1024]{0:T(1024)}, u32[]{:S(2)}) copy-start(s32[1024]{0:T(1024)} %copy-done.10) | copy-start | bytes 12292
  536.6 99.4 %copy-start.22 = (s32[16]{0:T(128)S(1)}, s32[16]{0:T(128)}, u32[]{:S(2)}) copy-start(s32[16]{0:T(128)} %copy-done.21) | copy-start | bytes 196
Sparse Core Ops, SparseCore 0:
  536.7 95.9 all-reduce.1
where the time goes:
time: 649 us; the launch traced here: 646 us
  waiting for transfers between devices  357 us (55%)
  matrix products  87.6 us (13%)
  local copies, waits for them, and re-layouts  66.9 us (10%)
  other arithmetic  56 us (9%)
  blocking collectives  31.1 us (5%)
  starting transfers between devices  29.7 us (5%)
  between operations  17.2 us (3%)
    all_to_all x1, waiting for transfers between devices, body(): lax.all_to_all(sums, 'blk', split_axis=0, concat_axis=0, tiled=True)  171 us
    psum x1, waiting for transfers between devices, body(): whole_sum = lax.psum(partial_update, 'head')  96.1 us
    all_to_all x1, waiting for transfers between devices, body(): lax.all_to_all(send_q, 'blk', split_axis=0, concat_axis=0, tiled=True)  89.9 us
    dot_general x16, matrix products, one_block(): jnp.einsum('thd,rhd->htr', block_q, cache_keys, preferred_element_type=jn...  39.2 us
    dot_general x16, matrix products, one_block(): jnp.einsum('htr,rhd->thd', weights, cache_values, preferred_element_type=...  26.9 us
    reduce_sum x17, other arithmetic, softmax_part(): return (peak, jnp.sum(weights, axis=-1), weights.astype(jnp.bfloat16))  24 us
    dynamic_update_slice x48, local copies, waits for them, and re-layouts, cache_part(): maxima, totals, sums = lax.map(one_block, (flat_q, flat_var))  16.9 us
    all_to_all x1, blocking collectives, body(): lax.all_to_all(totals, 'blk', split_axis=0, concat_axis=0, tiled=True)  16.1 us
  transfers between devices with their start and end apart: 4, of which 3 were waited for; matrix products, arithmetic and copies ran while one was open for 4% of the time, Pallas kernels for 0%

commit v1 on v0

v1 whole, which is shorter than its diff:
```python
import functools

import jax
import jax.numpy as jnp
from jax import lax
from jax.experimental import pallas as pl
from jax.experimental.pallas import tpu as pltpu
from jax.sharding import Mesh, PartitionSpec as P

DH = 64
F32 = jnp.float32
BF16 = jnp.bfloat16
NEG = -1e30
ANY = pl.ANY
BLK = ("y", "z", "c")


def remote(src, dst, send_sem, recv_sem, **device):
    return pltpu.make_async_remote_copy(
        src_ref=src,
        dst_ref=dst,
        send_sem=send_sem,
        recv_sem=recv_sem,
        device_id=device,
        device_id_type=pl.DeviceIdType.MESH,
    )


def each(count, first, step):
    def run(i, carry):
        step(i)
        return carry

    lax.fori_loop(first, count, run, 0)


def local_kernel(order, x_ref, wq_ref, wk_ref, wv_ref, cos_ref, sin_ref, qf_ref, kf_ref,
                 q_out, o_out, st_out, wide):
    x = x_ref[...]
    rows, cols = x.shape[0], wq_ref.shape[1]
    lane = lax.broadcasted_iota(jnp.int32, (rows, cols), 1)
    low = (lane % DH) < DH // 2
    cosine = jnp.concatenate([cos_ref[...]] * (cols // 128), axis=1)
    sine = jnp.concatenate([sin_ref[...]] * (cols // 128), axis=1)

    def turn(w_ref):
        a = jnp.dot(x, w_ref[...], preferred_element_type=F32)
        other = jnp.where(low, pltpu.roll(a, cols - DH // 2, 1), pltpu.roll(a, DH // 2, 1))
        return a * cosine + other * sine

    q = (turn(wq_ref) * 0.125).astype(BF16)
    k = turn(wk_ref).astype(BF16)
    v = jnp.dot(x, wv_ref[...], preferred_element_type=F32).astype(BF16)
    q_out[0] = q
    kf = kf_ref[...]
    half = lax.broadcasted_iota(jnp.int32, (rows, 128), 1)
    stats = jnp.zeros((rows, 128), F32)
    for pair in range(cols // 128):
        tile = slice(pair * 128, pair * 128 + 128)
        outs = []
        for odd in range(2):
            mine = (half >= DH) if odd else (half < DH)
            qa = jnp.where(mine, q[:, tile], qf_ref[:, tile])
            ka = jnp.where(mine, k[:, tile], kf)
            s = lax.dot_general(qa, ka, (((1,), (1,)), ((), ())), preferred_element_type=F32)
            m = jnp.max(s, axis=1, keepdims=True)
            p = jnp.exp(s - m)
            l = jnp.sum(p, axis=1, keepdims=True)
            o = jnp.dot(p.astype(BF16), v[:, tile], preferred_element_type=F32)
            outs.append(o / l)
            head = 2 * pair + odd
            stats = jnp.where(half == head, m, jnp.where(half == 4 + head, l, stats))
        o_out[0, :, tile] = jnp.where(half < DH, outs[0], outs[1])
    wide[...] = stats
    st_out[0] = jnp.transpose(wide[...])[:8]


def cache_kernel(q_ref, qf_ref, k_ref, kf_ref, v_ref, o_ref, st_ref, wide):
    pair, tile, odd = pl.program_id(0), pl.program_id(1), pl.program_id(2)
    rows, keys = q_ref.shape[0], k_ref.shape[0]
    lane_q = lax.broadcasted_iota(jnp.int32, (rows, 128), 1)
    lane_k = lax.broadcasted_iota(jnp.int32, (keys, 128), 1)
    mine_q = (lane_q // DH) == odd
    mine_k = (lane_k // DH) == odd
    qa = jnp.where(mine_q, q_ref[...], qf_ref[...])
    ka = jnp.where(mine_k, k_ref[...], kf_ref[...])
    s = lax.dot_general(qa, ka, (((1,), (1,)), ((), ())), preferred_element_type=F32)
    m = jnp.max(s, axis=1, keepdims=True)
    p = jnp.exp(s - m)
    l = jnp.sum(p, axis=1, keepdims=True)
    o = jnp.dot(p.astype(BF16), v_ref[...], preferred_element_type=F32) / l

    @pl.when(odd == 0)
    def _():
        o_ref[...] = o.astype(BF16)

    @pl.when(odd == 1)
    def _():
        o_ref[...] = jnp.where(mine_q, o, o_ref[...].astype(F32)).astype(BF16)

    head = 2 * pair + odd
    here = pl.ds(pl.multiple_of(tile * rows, rows), rows)
    wide[here, :] = jnp.where(
        lane_q == head, m, jnp.where(lane_q == 4 + head, l, wide[here, :])
    )

    @pl.when((pair == pl.num_programs(0) - 1) & (tile == pl.num_programs(1) - 1) & (odd == 1))
    def _():
        for slot in range(st_ref.shape[0]):
            st_ref[slot] = jnp.transpose(wide[slot * 128:slot * 128 + 128, :])[:8]


def spread_kernel(sizes, inv, ck, cv, q, kv, qh, abuf, bbuf, gbuf,
                  s_a, r_a, s_b, r_b, s_g, r_g, s_q, r_q, s_r, s_l, r_l, r_r, s_fr, s_fl, r_fl, r_fr,
                  s_s, r_s, here):
    X, Y, Z, C = sizes
    y, z, c = lax.axis_index("y"), lax.axis_index("z"), lax.axis_index("c")
    W = Y * C
    w = y * C + c
    bpq = kv.shape[3]
    barrier = pltpu.get_barrier_semaphore()

    def greet_cluster(i):
        other = (w + i) % W
        pl.semaphore_signal(barrier, inc=1, device_id={"y": other // C, "c": other % C},
                            device_id_type=pl.DeviceIdType.MESH)

    def greet_line(i):
        pl.semaphore_signal(barrier, inc=1, device_id={"z": (z + i) % Z},
                            device_id_type=pl.DeviceIdType.MESH)

    each(W, 1, greet_cluster)
    each(Z, 1, greet_line)
    pl.semaphore_wait(barrier, W - 1 + Z - 1)

    def first(kind, step):
        to = (y + step) % Y
        src = (ck, cv)[kind].at[to]
        return to, src

    for step in range(1, Y):
        for kind in range(C):
            to, src = first(kind, step)
            remote(src, abuf.at[w], s_a.at[to * C + kind], r_a.at[w], y=to, c=kind).start()
    for kind in range(C):
        _, src = first(kind, 0)

        @pl.when(kind != c)
        def _():
            remote(src, abuf.at[w], s_a.at[y * C + kind], r_a.at[w], c=kind).start()

        @pl.when(kind == c)
        def _():
            pltpu.make_async_copy(src, abuf.at[w], here.at[0]).start()

    def send_q(i):
        to = (z + i) % Z
        remote(q.at[to], qh.at[z], s_q.at[to], r_q.at[z], z=to).start()

    each(Z, 1, send_q)
    pltpu.make_async_copy(q.at[z], qh.at[z], here.at[1]).start()
    pltpu.make_async_copy(ck.at[y], abuf.at[w], here.at[0]).wait()

    def wait_a(i):
        src = (w + i) % W
        remote(abuf.at[src], abuf.at[src], s_a.at[src], r_a.at[src], y=src // C, c=src % C).wait_recv()

    each(W, 1, wait_a)

    def send_b(i):
        to = (z + i) % Z
        remote(abuf.at[:, to], bbuf.at[pl.ds(z * W, W)], s_b.at[to], r_b.at[z], z=to).start()

    each(Z, 1, send_b)
    own_b = pltpu.make_async_copy(abuf.at[:, z], bbuf.at[pl.ds(z * W, W)], here.at[2])
    own_b.start()
    own_b.wait()

    def wait_b(i):
        src = (z + i) % Z
        part = bbuf.at[pl.ds(src * W, W)]
        remote(part, part, s_b.at[src], r_b.at[src], z=src).wait_recv()

    each(Z, 1, wait_b)

    def pick(i):
        gbuf[i] = bbuf[inv[i]]

    each(Z * bpq, 0, pick)

    def send_g(i):
        to = (z + i) % Z
        remote(gbuf.at[pl.ds(to * bpq, bpq)], kv.at[c, y, z], s_g.at[to], r_g.at[z], z=to).start()

    own_g = pltpu.make_async_copy(gbuf.at[pl.ds(z * bpq, bpq)], kv.at[c, y, z], here.at[3])
    own_g.start()
    each(Z, 1, send_g)
    own_g.wait()

    right, left, far, twin = (y + 1) % Y, (y + Y - 1) % Y, (y + 2) % Y, 1 - c

    def to_twin(piece, at):
        return remote(kv.at[c, piece, at], kv.at[c, piece, at], s_s.at[piece, at], r_s.at[piece, at], c=twin)

    def from_twin(piece, at):
        part = kv.at[twin, piece, at]
        return remote(part, part, s_s.at[piece, at], r_s.at[piece, at], c=twin)

    def to_right(at):
        return remote(kv.at[c, y, at], kv.at[c, y, at], s_r.at[at], r_l.at[at], y=right)

    def to_left(at):
        return remote(kv.at[c, y, at], kv.at[c, y, at], s_l.at[at], r_r.at[at], y=left)

    def from_left(at):
        return remote(kv.at[c, left, at], kv.at[c, left, at], s_r.at[at], r_l.at[at], y=left)

    def from_right(at):
        return remote(kv.at[c, right, at], kv.at[c, right, at], s_l.at[at], r_r.at[at], y=right)

    def pass_right(at):
        return remote(kv.at[c, left, at], kv.at[c, left, at], s_fr.at[at], r_fl.at[at], y=right)

    def pass_left(at):
        return remote(kv.at[c, right, at], kv.at[c, right, at], s_fl.at[at], r_fr.at[at], y=left)

    def far_left(at):
        return remote(kv.at[c, far, at], kv.at[c, far, at], s_fr.at[at], r_fl.at[at], y=left)

    def far_right(at):
        return remote(kv.at[c, far, at], kv.at[c, far, at], s_fl.at[at], r_fr.at[at], y=right)

    def share(at):
        to_right(at).start()
        to_left(at).start()
        to_twin(y, at).start()

    def step1(i):
        at = (z + i) % Z
        remote(kv.at[c, y, at], kv.at[c, y, at], s_g.at[at], r_g.at[at], z=at).wait_recv()
        share(at)

    def step2(i):
        at = (z + i) % Z
        from_left(at).wait_recv()

        @pl.when(at % 2 == 0)
        def _():
            pass_right(at).start()

        to_twin(left, at).start()
        from_right(at).wait_recv()

        @pl.when(at % 2 == 1)
        def _():
            pass_left(at).start()

        to_twin(right, at).start()

    def step3(i):
        at = (z + i) % Z

        @pl.when(at % 2 == 0)
        def _():
            far_left(at).wait_recv()

        @pl.when(at % 2 == 1)
        def _():
            far_right(at).wait_recv()

        to_twin(far, at).start()

    share(z)

    def steps12(i):
        step1(i)
        step2(i - 1)

    each(Z, 1, steps12)
    step2(Z - 1)
    each(Z, 0, step3)

    def twins(i):
        for piece in range(Y):
            from_twin(piece, i).wait_recv()

    each(Z, 0, twins)

    def end_line(i):
        at = (z + i) % Z
        remote(q.at[at], qh.at[at], s_q.at[at], r_q.at[at], z=at).wait_recv()
        remote(q.at[at], qh.at[at], s_q.at[at], r_q.at[at], z=at).wait_send()
        remote(abuf.at[:, at], bbuf.at[pl.ds(at * W, W)], s_b.at[at], r_b.at[at], z=at).wait_send()
        part = gbuf.at[pl.ds(at * bpq, bpq)]
        remote(part, part, s_g.at[at], r_g.at[at], z=at).wait_send()

    each(Z, 1, end_line)
    pltpu.make_async_copy(q.at[z], qh.at[z], here.at[1]).wait()

    def end_cluster(i):
        to = (w + i) % W
        remote(abuf.at[to], abuf.at[to], s_a.at[to], r_a.at[to], y=to // C, c=to % C).wait_send()

    each(W, 1, end_cluster)

    def end_ring(at):
        to_right(at).wait_send()
        to_left(at).wait_send()

        @pl.when(at % 2 == 0)
        def _():
            pass_right(at).wait_send()

        @pl.when(at % 2 == 1)
        def _():
            pass_left(at).wait_send()

        for piece in range(Y):
            to_twin(piece, at).wait_send()

    each(Z, 0, end_ring)


def return_kernel(sizes, oh, sth, os, sts, attg, ro, rst, att,
                  s_o, r_o, s_t, r_t, s_r, s_l, r_l, r_r, s_fr, s_fl, r_fl, r_fr, here, mine):
    X, Y, Z, C = sizes
    x, z = lax.axis_index("x"), lax.axis_index("z")
    right, left, far = (x + 1) % X, (x + X - 1) % X, (x + 2) % X
    rows, cols = ro.shape[1], ro.shape[2]
    half = rows // 2
    barrier = pltpu.get_barrier_semaphore()

    def greet_line(i):
        pl.semaphore_signal(barrier, inc=1, device_id={"z": (z + i) % Z},
                            device_id_type=pl.DeviceIdType.MESH)

    each(Z, 1, greet_line)
    for side in (right, left):
        pl.semaphore_signal(barrier, inc=1, device_id={"x": side}, device_id_type=pl.DeviceIdType.MESH)
    pl.semaphore_wait(barrier, Z - 1 + 2)

    def send(i):
        to = (z + i) % Z
        remote(oh.at[to], ro.at[z], s_o.at[to], r_o.at[z], z=to).start()
        remote(sth.at[to], rst.at[z], s_t.at[to], r_t.at[z], z=to).start()

    own_o = pltpu.make_async_copy(oh.at[z], ro.at[z], here.at[0])
    own_t = pltpu.make_async_copy(sth.at[z], rst.at[z], here.at[1])
    own_o.start()
    own_t.start()
    each(Z, 1, send)
    lane = lax.broadcasted_iota(jnp.int32, (8, cols), 1)
    row = lax.broadcasted_iota(jnp.int32, (8, cols), 0)
    widen = jnp.where(lane // DH == row, 1.0, 0.0).astype(F32)

    def keep(at):
        return pltpu.make_async_copy(att.at[at], attg.at[x, at], mine.at[at])

    def to_right(at):
        return remote(att.at[at], attg.at[x, at], s_r.at[at], r_l.at[at], x=right)

    def to_left(at):
        return remote(att.at[at], attg.at[x, at], s_l.at[at], r_r.at[at], x=left)

    def from_left(at):
        return remote(att.at[at], attg.at[left, at], s_r.at[at], r_l.at[at], x=left)

    def from_right(at):
        return remote(att.at[at], attg.at[right, at], s_l.at[at], r_r.at[at], x=right)

    def part(who, at, side):
        return attg.at[who, at, pl.ds(side * half, half)]

    def pass_right(at):
        return remote(part(left, at, 0), part(left, at, 0), s_fr.at[at], r_fl.at[at], x=right)

    def pass_left(at):
        return remote(part(right, at, 1), part(right, at, 1), s_fl.at[at], r_fr.at[at], x=left)

    def far_left(at):
        return remote(part(far, at, 0), part(far, at, 0), s_fr.at[at], r_fl.at[at], x=left)

    def far_right(at):
        return remote(part(far, at, 1), part(far, at, 1), s_fl.at[at], r_fr.at[at], x=right)

    def join(at):
        far_m, far_l = rst[at][0:4], rst[at][4:8]
        own_m, own_l = sts[at][0:4], sts[at][4:8]
        m = jnp.maximum(far_m, own_m)
        a = far_l * jnp.exp(far_m - m)
        b = own_l * jnp.exp(own_m - m)
        total = a + b
        zero = jnp.zeros_like(total)

        def wide(share):
            return lax.dot_general(
                jnp.concatenate([share, zero], axis=0), widen, (((0,), (0,)), ((), ())),
                preferred_element_type=F32, precision=lax.Precision.HIGHEST)

        value = wide(a / total) * ro[at].astype(F32) + wide(b / total) * os[at]
        att[at] = value.astype(BF16)
        keep(at).start()
        to_right(at).start()
        to_left(at).start()

    def arrive(i):
        at = (z + i) % Z
        remote(oh.at[at], ro.at[at], s_o.at[at], r_o.at[at], z=at).wait_recv()
        remote(sth.at[at], rst.at[at], s_t.at[at], r_t.at[at], z=at).wait_recv()
        join(at)

    def forward(i):
        at = (z + i) % Z
        from_left(at).wait_recv()
        pass_right(at).start()
        from_right(at).wait_recv()
        pass_left(at).start()

    own_o.wait()
    own_t.wait()
    join(z)

    def steps(i):
        arrive(i)
        forward(i - 1)

    each(Z, 1, steps)
    forward(Z - 1)

    def finish(at):
        far_left(at).wait_recv()
        far_right(at).wait_recv()
        keep(at).wait()
        to_right(at).wait_send()
        to_left(at).wait_send()
        pass_right(at).wait_send()
        pass_left(at).wait_send()

    each(Z, 0, finish)

    def end_line(i):
        at = (z + i) % Z
        remote(oh.at[at], ro.at[at], s_o.at[at], r_o.at[at], z=at).wait_send()
        remote(sth.at[at], rst.at[at], s_t.at[at], r_t.at[at], z=at).wait_send()

    each(Z, 1, end_line)


def out_kernel(where, att_ref, w_ref, x_ref, gain_ref, sel_ref, upd_ref, pool_ref, y_ref):
    parts, cols = att_ref.shape[0], att_ref.shape[3]
    y = jnp.dot(att_ref[0, 0], w_ref[0:cols, :], preferred_element_type=F32)
    for p in range(1, parts):
        y += jnp.dot(att_ref[p, 0], w_ref[p * cols:(p + 1) * cols, :], preferred_element_type=F32)
    y_ref[...] = y
    mine = where[where.shape[0] - 1]
    upd_ref[...] = y_ref[:, pl.ds(pl.multiple_of(mine * cols, cols), cols)]
    hidden = x_ref[...].astype(F32) + y
    square = jnp.sum(hidden * hidden, axis=1, keepdims=True)
    weighted = jnp.sum(hidden * gain_ref[...], axis=1, keepdims=True)
    score = weighted * lax.rsqrt(square / y.shape[1] + 1e-06)
    pool_ref[0] = jnp.dot(sel_ref[0], jnp.broadcast_to(score, (score.shape[0], 128)),
                          preferred_element_type=F32, precision=lax.Precision.HIGHEST)


def body(sizes, doc_x, doc_seg, doc_query, doc_var, query_len, block_perm, cache_k, cache_v, cache_var,
         w_query, w_key, w_value, w_out, var_bias, norm_gain, readout):
    X, Y, Z, C = sizes
    W = Y * C
    tokens, cols = doc_x.shape[0], w_query.shape[1]
    features = doc_x.shape[1]
    heads = cols // DH
    slot = tokens // Z
    crows = cache_k.shape[0]
    blocks = Y * Z * C
    bpq = blocks // Z
    keys = bpq * crows
    x_id, z_id, blk = lax.axis_index("x"), lax.axis_index("z"), lax.axis_index(BLK)
    i32 = jnp.int32
    iz = jnp.arange(Z, dtype=i32)

    w_all = lax.all_gather(w_out, "x", axis=0, tiled=True)

    slot_query = lax.dynamic_slice_in_dim(doc_query, blk * 2 * Z, 2 * Z).reshape(Z, 2)[:, 0]
    match = (slot_query[None, :] == iz[:, None]).astype(i32)
    order = jnp.sum(match * iz[None, :], axis=1)
    seg = doc_seg.reshape(Z, slot) - blk * (2 * Z) - 2 * iz[:, None]
    first_len = jnp.sum((seg == 0).astype(i32), axis=1)
    offset = jnp.arange(slot, dtype=i32)[None, :] - seg * first_len[:, None]
    packed = jnp.stack([seg, offset, doc_var.reshape(Z, slot)])
    packed = jnp.sum(jnp.where(match[None, :, :, None] == 1, packed[:, None], 0), axis=2)
    seg_q, off_q, var_q = packed[0], packed[1], packed[2]
    positions = (query_len[:, None] + off_q).reshape(tokens)

    payload = jnp.concatenate([cache_var, var_q.reshape(tokens)])
    everyone = lax.all_gather(payload, BLK)

    lane = jnp.arange(128, dtype=i32)
    half_size = DH // 2
    frequency = 10000.0 ** (-jnp.arange(half_size, dtype=F32) / half_size)
    angles = positions.astype(F32)[:, None] * jnp.tile(frequency, 128 // half_size)[None, :]
    cosine = jnp.cos(angles)
    sine = jnp.where((lane % DH < half_size)[None, :], -jnp.sin(angles), jnp.sin(angles))

    feature = lane % DH
    delta = var_bias[0] - var_bias[1]
    hi = lax.reduce_precision(delta, 8, 7)
    mid = lax.reduce_precision(delta - hi, 8, 7)
    low = lax.reduce_precision(delta - hi - mid, 8, 7)
    parts = jnp.stack([hi, mid, low])
    swapped = parts.reshape(3, heads // 2, 2)[:, :, ::-1].reshape(3, heads)
    col = jnp.arange(cols, dtype=i32)
    col_feature = col % DH
    per_col = jnp.repeat(swapped, DH, axis=1)
    table = jnp.where(col_feature < 8, per_col[0],
                      jnp.where(col_feature < 16, per_col[1], jnp.where(col_feature < 24, per_col[2], 0.0)))

    def query_features(var, segment):
        same = (var[:, None] == (col_feature % 8)[None, :])
        value = jnp.where(same, table[None, :], 0.0)
        value = jnp.where((col_feature == 24)[None, :], 1.0, value)
        if segment is not None:
            value = jnp.where((col_feature[None, :] - 25) == segment[:, None], 1.0, value)
        return value.astype(BF16)

    def key_features(var, valid, segment):
        same = (var[:, None] == (feature % 8)[None, :]) & (feature < 24)[None, :]
        value = jnp.where(same, 1.0, 0.0)
        if valid is not None:
            value = jnp.where((feature == 24)[None, :] & ~valid[:, None], NEG, value)
        if segment is not None:
            f = feature[None, :] - 25
            value = jnp.where(((f == 0) | (f == 1)) & (f != segment[:, None]), NEG, value)
        return value.astype(BF16)

    seg_flat, var_flat = seg_q.reshape(tokens), var_q.reshape(tokens)
    qf = query_features(var_flat, seg_flat)
    kf = key_features(var_flat, None, seg_flat)

    full = lambda *shape: pl.BlockSpec(shape, lambda i, *_: (0,) * len(shape))
    q_rot, own_o, own_st = pl.pallas_call(
        local_kernel,
        grid_spec=pltpu.PrefetchScalarGridSpec(
            num_scalar_prefetch=1,
            grid=(Z,),
            in_specs=[
                pl.BlockSpec((slot, features), lambda i, o: (o[i], 0)),
                full(features, cols), full(features, cols), full(features, cols),
                pl.BlockSpec((slot, 128), lambda i, o: (i, 0)),
                pl.BlockSpec((slot, 128), lambda i, o: (i, 0)),
                pl.BlockSpec((slot, cols), lambda i, o: (i, 0)),
                pl.BlockSpec((slot, 128), lambda i, o: (i, 0)),
            ],
            out_specs=[
                pl.BlockSpec((1, slot, cols), lambda i, o: (i, 0, 0)),
                pl.BlockSpec((1, slot, cols), lambda i, o: (i, 0, 0)),
                pl.BlockSpec((1, 8, slot), lambda i, o: (i, 0, 0)),
            ],
            scratch_shapes=[pltpu.VMEM((slot, 128), F32)],
        ),
        out_shape=[
            jax.ShapeDtypeStruct((Z, slot, cols), BF16),
            jax.ShapeDtypeStruct((Z, slot, cols), F32),
            jax.ShapeDtypeStruct((Z, 8, slot), F32),
        ],
        compiler_params=pltpu.CompilerParams(vmem_limit_bytes=32 << 20),
        name="local_part",
    )(order, doc_x, w_query, w_key, w_value, cosine, sine, qf, kf)

    by_block = jnp.sum(
        jnp.where(block_perm[None, :] == jnp.arange(blocks, dtype=i32)[:, None],
                  jnp.arange(blocks, dtype=i32)[None, :], 0), axis=1)
    inv = (by_block // C % Z) * W + (by_block // (Z * C)) * C + by_block % C

    dma = pltpu.SemaphoreType.DMA
    piece = crows // (Y * Z)
    kv, q_home = pl.pallas_call(
        functools.partial(spread_kernel, sizes),
        in_specs=[pl.BlockSpec(memory_space=pltpu.SMEM)] + [pl.BlockSpec(memory_space=ANY)] * 3,
        out_specs=[pl.BlockSpec(memory_space=ANY)] * 2,
        out_shape=[
            jax.ShapeDtypeStruct((C, Y, Z, bpq, piece, cols), BF16),
            jax.ShapeDtypeStruct((Z, slot, cols), BF16),
        ],
        scratch_shapes=[
            pltpu.VMEM((W, Z, piece, cols), BF16),
            pltpu.VMEM((Z * W, piece, cols), BF16),
            pltpu.VMEM((Z * bpq, piece, cols), BF16),
            dma((W,)), dma((W,)), dma((Z,)), dma((Z,)), dma((Z,)), dma((Z,)), dma((Z,)), dma((Z,)),
            dma((Z,)), dma((Z,)), dma((Z,)), dma((Z,)), dma((Z,)), dma((Z,)), dma((Z,)), dma((Z,)),
            dma((Y, Z)), dma((Y, Z)), dma((4,)),
        ],
        compiler_params=pltpu.CompilerParams(
            collective_id=0, has_side_effects=True, vmem_limit_bytes=16 << 20),
        name="spread",
    )(inv, cache_k.reshape(Y, Z, piece, cols), cache_v.reshape(Y, Z, piece, cols), q_rot)

    mine = lax.dynamic_slice_in_dim(by_block, z_id * bpq, bpq)
    key_var = jnp.take(everyone[:, :crows], mine, axis=0)
    key_var = key_var.reshape(bpq, Y, Z, piece).transpose(1, 2, 0, 3).reshape(keys)
    position = (jnp.arange(bpq, dtype=i32)[None, None, :, None] * crows
                + jnp.arange(Y, dtype=i32)[:, None, None, None] * (Z * piece)
                + jnp.arange(Z, dtype=i32)[None, :, None, None] * piece
                + jnp.arange(piece, dtype=i32)[None, None, None, :]).reshape(keys)
    my_len = lax.dynamic_slice_in_dim(query_len, z_id, 1)[0]
    ckf = key_features(key_var, position < my_len, None)
    home_var = everyone[:, crows:].reshape(Y, Z, C, Z, slot)
    home_var = lax.dynamic_slice(
        home_var, (lax.axis_index("y"), 0, lax.axis_index("c"), z_id, 0), (1, Z, 1, 1, slot)).reshape(tokens)
    hqf = query_features(home_var, None)

    rows = 256
    o_home, st_home = pl.pallas_call(
        cache_kernel,
        grid=(heads // 2, tokens // rows, 2),
        in_specs=[
            pl.BlockSpec((rows, 128), lambda p, t, o: (t, p)),
            pl.BlockSpec((rows, 128), lambda p, t, o: (t, p)),
            pl.BlockSpec((keys, 128), lambda p, t, o: (0, p)),
            pl.BlockSpec((keys, 128), lambda p, t, o: (0, 0)),
            pl.BlockSpec((keys, 128), lambda p, t, o: (0, p)),
        ],
        out_specs=[
            pl.BlockSpec((rows, 128), lambda p, t, o: (t, p)),
            pl.BlockSpec((Z, 8, slot), lambda p, t, o: (0, 0, 0)),
        ],
        out_shape=[
            jax.ShapeDtypeStruct((tokens, cols), BF16),
            jax.ShapeDtypeStruct((Z, 8, slot), F32),
        ],
        scratch_shapes=[pltpu.VMEM((tokens, 128), F32)],
        compiler_params=pltpu.CompilerParams(vmem_limit_bytes=56 << 20),
        name="cache_part",
    )(q_home.reshape(tokens, cols), hqf, kv[0].reshape(keys, cols), ckf, kv[1].reshape(keys, cols))

    attended = pl.pallas_call(
        functools.partial(return_kernel, sizes),
        in_specs=[pl.BlockSpec(memory_space=ANY)] * 2 + [pl.BlockSpec(memory_space=pltpu.VMEM)] * 2,
        out_specs=pl.BlockSpec(memory_space=ANY),
        out_shape=jax.ShapeDtypeStruct((X, Z, slot, cols), BF16),
        scratch_shapes=[
            pltpu.VMEM((Z, slot, cols), BF16),
            pltpu.VMEM((Z, 8, slot), F32),
            pltpu.VMEM((Z, slot, cols), BF16),
        ] + [dma((Z,))] * 12 + [dma((2,)), dma((Z,))],
        compiler_params=pltpu.CompilerParams(
            collective_id=1, has_side_effects=True, vmem_limit_bytes=16 << 20),
        name="give_back",
    )(o_home.reshape(Z, slot, cols), st_home, own_o, own_st)

    sel = jnp.stack([seg == 0, seg == 1], axis=1)
    share = jnp.where(sel, 1.0 / jnp.sum(sel.astype(F32), axis=2, keepdims=True), 0.0)
    share = jnp.concatenate([share, jnp.zeros((Z, 6, slot), F32)], axis=1)
    gain = (norm_gain * readout).reshape(1, features)
    where = jnp.concatenate([slot_query, x_id.reshape(1).astype(i32)])
    update, pooled = pl.pallas_call(
        out_kernel,
        grid_spec=pltpu.PrefetchScalarGridSpec(
            num_scalar_prefetch=1,
            grid=(Z,),
            in_specs=[
                pl.BlockSpec((X, 1, slot, cols), lambda i, w: (0, w[i], 0, 0)),
                full(X * cols, features),
                pl.BlockSpec((slot, features), lambda i, w: (i, 0)),
                full(1, features),
                pl.BlockSpec((1, 8, slot), lambda i, w: (i, 0, 0)),
            ],
            out_specs=[
                pl.BlockSpec((slot, cols), lambda i, w: (i, 0)),
                pl.BlockSpec((1, 8, 128), lambda i, w: (i, 0, 0)),
            ],
            scratch_shapes=[pltpu.VMEM((slot, features), F32)],
        ),
        out_shape=[
            jax.ShapeDtypeStruct((tokens, cols), F32),
            jax.ShapeDtypeStruct((Z, 8, 128), F32),
        ],
        compiler_params=pltpu.CompilerParams(vmem_limit_bytes=32 << 20),
        name="out_part",
    )(where, attended, w_all, doc_x, gain, share)
    return update, pooled[:, :2, 0].reshape(2 * Z)


def solution(mesh):
    heads = mesh.shape["head"]
    cores = 2
    across = 4
    along = mesh.shape["blk"] // (across * cores)
    sizes = (heads, across, along, cores)
    split = Mesh(mesh.devices.reshape(sizes), ("x", "y", "z", "c"))
    return jax.shard_map(
        functools.partial(body, sizes),
        mesh=split,
        in_specs=(
            P(BLK, None), P(BLK), P(), P(BLK), P(), P(),
            P(BLK, "x"), P(BLK, "x"), P(BLK),
            P(None, "x"), P(None, "x"), P(None, "x"), P("x", None), P(None, "x"),
            P(), P(),
        ),
        out_specs=(P(BLK, "x"), P(BLK)),
        check_vma=False,
    )
```

time: 649 us -> 290 us (0.45)
  waiting for transfers between devices: 357 us -> 0.68 us
  Pallas kernels: 0 us -> 163 us
  matrix products: 87.6 us -> 0 us
  other arithmetic: 56 us -> 24.1 us
  local copies, waits for them, and re-layouts: 66.9 us -> 36.8 us
  starting transfers between devices: 29.7 us -> 0.04 us
  blocking collectives: 31.1 us -> 50.5 us
    all_to_all x3 -> x0, waiting for transfers between devices: 260 us -> none  [the longest x1 171 us: body(): lax.all_to_all(sums, 'blk', split_axis=0, concat_axis=0, tiled=True)]
    pallas_call x0 -> x5, Pallas kernels: none -> 163 us  [the longest x1 66.4 us: body(): pl.pallas_call(functools.partial(spread_kernel, sizes), in_specs=[pl.Bloc...]
    psum x1 -> x0, waiting for transfers between devices: 96.1 us -> none  [body(): whole_sum = lax.psum(partial_update, 'head')]
    dot_general x43 -> x0, matrix products: 87.6 us -> none  [the longest x16 39.2 us: one_block(): jnp.einsum('thd,rhd->htr', block_q, cache_keys, preferred_element_type=jn...]
    all_gather x0 -> x1, blocking collectives: none -> 50.5 us  [body(): everyone = lax.all_gather(payload, BLK)]
    all_to_all x2 -> x0, blocking collectives: 31.1 us -> none  [the longest x1 16.1 us: body(): lax.all_to_all(totals, 'blk', split_axis=0, concat_axis=0, tiled=True)]
    all_to_all x3 -> x0, starting transfers between devices: 29.5 us -> none  [the longest x1 12.1 us: body(): lax.all_to_all(send_var, 'blk', split_axis=0, concat_axis=0, tiled=True)]
    reduce_sum x21 -> x5, other arithmetic: 28.2 us -> 3.2 us  [the longest x1 1.34 us: body(): jnp.sum(jnp.where(block_perm[None, :] == jnp.arange(blocks, dtype=i32)[:,...]
  transfers between devices with their start and end apart: 4 -> 1, of which waited for: 3 -> 0; matrix products, arithmetic and copies ran while one was open for 4% -> 18% of each run, Pallas kernels for 0% -> 54%
where the time goes in v1:
time: 290 us; the launch traced here: 289 us
  Pallas kernels  163 us (56%)
  blocking collectives  50.5 us (17%)
  local copies, waits for them, and re-layouts  36.8 us (13%)
  other arithmetic  24.1 us (8%)
  between operations  14.3 us (5%)
    pallas_call x1, Pallas kernels, body(): pl.pallas_call(functools.partial(spread_kernel, sizes), in_specs=[pl.Bloc...  66.4 us
    all_gather x1, blocking collectives, body(): everyone = lax.all_gather(payload, BLK)  50.5 us
    pallas_call x1, Pallas kernels, body(): pl.pallas_call(functools.partial(return_kernel, sizes), in_specs=[pl.Bloc...  44.3 us
    pallas_call x1, Pallas kernels, body(): pl.pallas_call(cache_kernel, grid=(heads // 2, tokens // rows, 2), in_spe...  33.8 us
    pallas_call x1, Pallas kernels, body(): pl.pallas_call(local_kernel, grid_spec=pltpu.PrefetchScalarGridSpec(num_s...  11.3 us
    unnamed x46, local copies, waits for them, and re-layouts  7.74 us
    broadcast_in_dim x6, local copies, waits for them, and re-layouts, body(): per_col = jnp.repeat(swapped, DH, axis=1)  7.7 us
    pallas_call x1, Pallas kernels, body(): pl.pallas_call(out_kernel, grid_spec=pltpu.PrefetchScalarGridSpec(num_sca...  7.27 us
  transfers between devices with their start and end apart: 1, of which 0 were waited for; matrix products, arithmetic and copies ran while one was open for 18% of the time, Pallas kernels for 54%

profile of v1, /device:TPU:8, one launch (start us, length us, event | category | flops | bytes accessed | tf_op | source)
XLA Modules:
  0.0 289.4 jit_solution(9707957455517994652)
XLA Ops:
  15.8 50.5 %all-gather.1 = s32[64,1,1536]{2,1,0:T(1,128)S(1)} all-gather(s32[1,1,1536]{2,1,0:T(1,128)S(1)} %reshape.457), channel_id=2, replica_groups=mesh['x'=4,'y'=4,'z'=8,'c'=2] {'y','z','c'}, dimensions={0}, use_global_device_ids=true | all-gather | bytes 399360 | tf_op jit(solution)/shard_map/all_gather | solution.py:495
  68.0 1.3 select_reduce_fusion.1
  69.4 1.2 tile.2
  70.6 1.3 mul.110
  71.9 1.4 fusion.8
  73.3 1.2 stack.21
  74.5 1.2 slice.66
  75.7 1.2 slice.67
  76.9 1.2 broadcast_in_dim.182
  78.1 1.3 broadcast_in_dim.183
  79.4 1.3 stack.22
  80.7 1.3 slice.68
  82.0 1.3 slice.69
  83.3 1.3 broadcast_in_dim.184
  84.5 1.3 broadcast_in_dim.185
  85.9 1.3 stack.23
  87.1 1.3 slice.70
  88.5 1.3 slice.71
  89.8 1.3 broadcast_in_dim.186
  91.0 1.4 broadcast_in_dim.187
  94.7 1.3 dynamic_slice.14
  104.0 2.6 negate_select_fusion
  106.6 1.5 select_convert_fusion.1
  108.1 11.3 %local_part.1 = (bf16[8,128,256]{2,1,0:T(8,128)(2,1)S(1)}, f32[8,128,256]{2,1,0:T(8,128)S(1)}, f32[8,8,128]{2,1,0:T(8,128)S(1)}) custom-call(s32[8]{0:T(128)S(1)} %select_reduce_fusion.2.order, bf16[1024,1024]{1,0:T(8,128)(2,1)S(1)} %copy-done, bf16[1024,256]{1,0:T(8,128)(2,1)S(1)} %copy-done.5, bf16[1024,256]{1,0:T(8,128)(2,1)S(1)} %copy-done.6, ...), custom_call_target="tpu_custom_call" | custom-call | tf_op jit(solution)/shard_map/local_part/pallas_call | solution.py:540
  119.4 66.4 %spread.1 = (bf16[2,4,8,8,16,256]{5,4,3,2,1,0:T(8,128)(2,1)S(1)}, bf16[8,128,256]{2,1,0:T(8,128)(2,1)S(1)}) custom-call(s32[64]{0:T(128)S(1)} %fusion.6.inv, bf16[4,8,16,256]{3,2,1,0:T(8,128)(2,1)S(1)} %bitcast.48, bf16[4,8,16,256]{3,2,1,0:T(8,128)(2,1)S(1)} %bitcast.49, bf16[8,128,256]{2,1,0:T(8,128)(2,1)S(1)} %get-tuple-element.11.q), custom_call_target="tpu_custom_call" | custom-call | tf_op jit(solution)/shard_map/spread/pallas_call | solution.py:576
  186.7 2.3 fusion.13
  189.0 2.4 select_convert_fusion.kf_ref
  191.4 33.8 %cache_part.1 = (bf16[1024,256]{1,0:T(8,128)(2,1)}, f32[8,8,128]{2,1,0:T(8,128)}) custom-call(bf16[1024,256]{1,0:T(8,128)(2,1)} %bitcast.46, bf16[1024,256]{1,0:T(8,128)(2,1)} %get-tuple-element.37.qf_ref, bf16[4096,256]{1,0:T(8,128)(2,1)} %bitcast.52, bf16[4096,128]{1,0:T(8,128)(2,1)} %select_convert_fusion.kf_ref, bf16[4096,256]{1,0:T(8,128)(2,1)} %bitcast.51), custom_call_target="tpu_custom_call" | custom-call | tf_op jit(solution)/shard_map/cache_part/pallas_call | solution.py:612
  227.0 44.3 %give_back.1.att_ref = bf16[4,8,128,256]{3,2,1,0:T(8,128)(2,1)S(1)} custom-call(bf16[8,128,256]{2,1,0:T(8,128)(2,1)S(1)} %bitcast.47, f32[8,8,128]{2,1,0:T(8,128)S(1)} %copy-done.10, f32[8,128,256]{2,1,0:T(8,128)S(1)} %get-tuple-element.16.os, f32[8,8,128]{2,1,0:T(8,128)S(1)} %get-tuple-element.17.sts), custom_call_target="tpu_custom_call" | custom-call | tf_op jit(solution)/shard_map/give_back/pallas_call | solution.py:635
  271.4 1.6 copy-done.1
  273.0 1.6 copy-done.2
  274.6 7.3 %out_part.1 = (f32[1024,256]{1,0:T(8,128)}, f32[8,8,128]{2,1,0:T(8,128)S(1)}) custom-call(s32[9]{0:T(128)S(1)} %pad_add_fusion.3.where, bf16[4,8,128,256]{3,2,1,0:T(8,128)(2,1)S(1)} %give_back.1.att_ref, bf16[1024,1024]{1,0:T(8,128)(2,1)S(1)} %copy-done.2, bf16[1024,1024]{1,0:T(8,128)(2,1)S(1)} %copy-done.1, f32[1,1024]{1,0:T(1,128)S(1)} %bitcast.50, ...), custom_call_target="tpu_custom_call" | custom-call | tf_op jit(solution)/shard_map/out_part/pallas_call | solution.py:655
  (94 shorter events, 24.0 us)
Async XLA Ops:
  7.2 264.2 %all-gather.4.cloned.1.call-start = ((), (), s32[]{:S(2)}) async-start(), calls=%async_computation | async-start | bytes 2621440 | tf_op jit(solution)/shard_map/all_gather | solution.py:481
  8.5 6.7 %copy-start.13 = (s32[8]{0:T(128)}, s32[8]{0:T(128)S(1)}, u32[]{:S(2)}) copy-start(s32[8]{0:T(128)S(1)} %iota_multiply_fusion.3) | copy-start | bytes 100
  11.7 0.6 copy-start.18
  13.2 0.6 copy-start.12
  66.4 41.7 %copy-start = (bf16[1024,1024]{1,0:T(8,128)(2,1)S(1)}, bf16[1024,1024]{1,0:T(8,128)(2,1)}, u32[]{:S(2)}) copy-start(bf16[1024,1024]{1,0:T(8,128)(2,1)} %x_ref.3) | copy-start | bytes 6291460
  66.4 41.7 %copy-start.5 = (bf16[1024,256]{1,0:T(8,128)(2,1)S(1)}, bf16[1024,256]{1,0:T(8,128)(2,1)}, u32[]{:S(2)}) copy-start(bf16[1024,256]{1,0:T(8,128)(2,1)} %wq_ref.1) | copy-start | bytes 1572868
  66.4 41.7 %copy-start.6 = (bf16[1024,256]{1,0:T(8,128)(2,1)S(1)}, bf16[1024,256]{1,0:T(8,128)(2,1)}, u32[]{:S(2)}) copy-start(bf16[1024,256]{1,0:T(8,128)(2,1)} %wk_ref.1) | copy-start | bytes 1572868
  93.1 13.5 %copy-start.11 = (s32[1024]{0:T(1024)S(1)}, s32[1024]{0:T(1024)}, u32[]{:S(2)}) copy-start(s32[1024]{0:T(1024)} %get-tuple-element.31) | copy-start | bytes 12292
  93.1 13.5 %copy-start.14 = (s32[256]{0:T(256)S(1)}, s32[256]{0:T(256)}, u32[]{:S(2)}) copy-start(s32[256]{0:T(256)} %get-tuple-element.39) | copy-start | bytes 3076
  93.1 13.5 %copy-start.15 = (s32[256]{0:T(256)S(1)}, s32[256]{0:T(256)}, u32[]{:S(2)}) copy-start(s32[256]{0:T(256)} %get-tuple-element.40) | copy-start | bytes 3076
  99.2 8.9 %copy-start.7 = (bf16[1024,256]{1,0:T(8,128)(2,1)S(1)}, bf16[1024,256]{1,0:T(8,128)(2,1)}, u32[]{:S(2)}) copy-start(bf16[1024,256]{1,0:T(8,128)(2,1)} %wv_ref.1) | copy-start | bytes 1572868
  108.1 11.3 %copy-start.20 = (s32[64]{0:T(128)S(1)}, s32[64]{0:T(128)}, u32[]{:S(2)}) copy-start(s32[64]{0:T(128)} %select_reduce_fusion.1) | copy-start | bytes 772
  108.1 11.3 %copy-start.8 = (bf16[512,256]{1,0:T(8,128)(2,1)S(1)}, bf16[512,256]{1,0:T(8,128)(2,1)}, u32[]{:S(2)}) copy-start(bf16[512,256]{1,0:T(8,128)(2,1)} %param.22) | copy-start | bytes 786436
  108.1 11.3 %copy-start.9 = (bf16[512,256]{1,0:T(8,128)(2,1)S(1)}, bf16[512,256]{1,0:T(8,128)(2,1)}, u32[]{:S(2)}) copy-start(bf16[512,256]{1,0:T(8,128)(2,1)} %param.23) | copy-start | bytes 786436
  185.9 0.8 copy-start.3
  186.7 2.3 copy-start.16
  186.7 2.3 copy-start.17
  225.2 46.1 %copy-start.19 = (s32[8]{0:T(128)S(1)}, s32[8]{0:T(128)}, u32[]{:S(2)}) copy-start(s32[8]{0:T(128)} %copy-done.18) | copy-start | bytes 100
  225.2 1.0 copy-start.4
  226.2 0.8 copy-start.10
  271.4 1.6 copy-start.1
  273.0 1.6 copy-start.2
Sparse Core Ops, SparseCore 0:
  9.8 36.2 all-gather.3

commit v2 on v0

v2 whole, which is shorter than its diff:
```python
import functools

import jax
import jax.numpy as jnp
import numpy as np
from jax import lax
from jax.experimental import pallas as pl
from jax.experimental.pallas import tpu as pltpu
from jax.sharding import Mesh, PartitionSpec as P

DH = 64
F32 = jnp.float32
BF16 = jnp.bfloat16
NEG = -1e30
ANY = pl.ANY
BLK = ("y", "z", "c")


def remote(src, dst, send_sem, recv_sem, **device):
    return pltpu.make_async_remote_copy(
        src_ref=src,
        dst_ref=dst,
        send_sem=send_sem,
        recv_sem=recv_sem,
        device_id=device,
        device_id_type=pl.DeviceIdType.MESH,
    )


def each(count, first, step):
    def run(i, carry):
        step(i)
        return carry

    lax.fori_loop(first, count, run, 0)


def nth_near(i, Z):
    return lax.rem(jnp.where(i % 2 == 1, (i + 1) // 2, Z - i // 2), Z)


def attention_kernel(
    sizes, inv, dq, qlen, bias, seg_ref, var_ref, tcos_ref, tsin_ref, freq_ref, x_in, wq_in, wk_in, wv_in,
    ck, cv, cvar, attg,
    xv, wq, wk, wv, order, abuf, bbuf, gbuf, va, vb, kv, qrot, qh, dv, hv, cosv, sinv, qtab, ktab,
    os, sts, ka, vx, qa, acc, mx, oh, sth, ro, rst, att,
    s_x, s_a, r_a, s_va, r_va, s_b, r_b, s_vb, r_vb, s_g, r_g, s_q, r_q, s_dv, r_dv,
    s_r, s_l, r_l, r_r, s_fr, s_fl, r_fl, r_fr, s_s, r_s,
    s_o, r_o, s_t, r_t, x_r, x_l, y_l, y_r, x_fr, x_fl, y_fl, y_fr, mine_sem, here,
):
    X, Y, Z, C = sizes
    x, y, z, c = lax.axis_index("x"), lax.axis_index("y"), lax.axis_index("z"), lax.axis_index("c")
    W = Y * C
    w = y * C + c
    bpq = W
    blk = (y * Z + z) * C + c
    slot, cols = qrot.shape[1], qrot.shape[2]
    heads = cols // DH
    pairs = cols // 128
    part_keys = bpq * slot
    barrier = pltpu.get_barrier_semaphore()

    loads = [pltpu.make_async_copy(s, d, s_x.at[n]) for n, (s, d) in
             enumerate(((x_in, xv), (wq_in, wq), (wk_in, wk), (wv_in, wv)))]
    for load in loads:
        load.start()

    def greet(**device):
        pl.semaphore_signal(barrier, inc=1, device_id=device, device_id_type=pl.DeviceIdType.MESH)

    each(W, 1, lambda i: greet(y=(w + i) % W // C, c=(w + i) % W % C))
    each(Z, 1, lambda i: greet(z=(z + i) % Z))
    for side in ((x + 1) % X, (x + X - 1) % X):
        greet(x=side)

    slot_query = [dq[blk * 2 * Z + 2 * j] for j in range(Z)]
    for query in range(Z):
        at = jnp.int32(0)
        for j in range(Z):
            at = jnp.where(slot_query[j] == query, j, at)
        order[query] = at
    lane2 = lax.broadcasted_iota(jnp.int32, (16, cols), 1)
    row2 = lax.broadcasted_iota(jnp.int32, (16, cols), 0)
    feat2 = lane2 % DH
    lane_head = 2 * (lane2 // 128) + (1 - lane2 % 128 // DH)
    delta = jnp.zeros((16, cols), F32)
    for h in range(heads):
        delta = jnp.where(lane_head == h, bias[0, h] - bias[1, h], delta)
    hi = delta.astype(BF16).astype(F32)
    mid = (delta - hi).astype(BF16).astype(F32)
    low = delta - hi - mid
    value = jnp.where(feat2 < 8, hi, jnp.where(feat2 < 16, mid, low))
    value = jnp.where((feat2 < 24) & (feat2 % 8 == row2), value, 0.0)
    qtab[...] = jnp.where((row2 >= 8) & (row2 < 11) & (feat2 == row2 + 16), 1.0, value).astype(BF16)
    lane1, row1 = lane2[:, :128], row2[:, :128]
    feat1 = lane1 % DH
    value = jnp.where((feat1 < 24) & (feat1 % 8 == row1), 1.0, 0.0)
    hit = (((row1 == 8) & (feat1 == 24)) | ((row1 == 9) & (feat1 == 26)) | ((row1 == 10) & (feat1 == 25)))
    ktab[...] = jnp.where(hit, NEG, value).astype(BF16)

    def features(rows, table):
        return lax.dot_general(rows.astype(BF16), table, (((0,), (0,)), ((), ())),
                               preferred_element_type=F32).astype(BF16)

    def marks(var, eight, seg):
        same = jnp.where((row1 < 8) & (var == row1), 1.0, 0.0)
        rows = jnp.where(row1 == 8, eight, same)
        if seg is not None:
            rows = jnp.where(((row1 == 9) & (seg == 0)) | ((row1 == 10) & (seg == 1)), 1.0, rows)
        return rows

    pl.semaphore_wait(barrier, W - 1 + Z - 1 + 2)

    for step in range(1, Y):
        to = (y + step) % Y
        for kind in range(C):
            remote((ck, cv)[kind].at[to], abuf.at[w], s_a.at[to * C + kind], r_a.at[w], y=to, c=kind).start()
            remote(cvar, va.at[w], s_va.at[to * C + kind], r_va.at[w], y=to, c=kind).start()
    for kind in range(C):
        src = (ck, cv)[kind].at[y]

        @pl.when(kind != c)
        def _():
            remote(src, abuf.at[w], s_a.at[y * C + kind], r_a.at[w], c=kind).start()
            remote(cvar, va.at[w], s_va.at[y * C + kind], r_va.at[w], c=kind).start()

        @pl.when(kind == c)
        def _():
            pltpu.make_async_copy(src, abuf.at[w], here.at[0]).start()

    own_var = pltpu.make_async_copy(cvar, va.at[w], here.at[1])
    own_var.start()

    lane = lax.broadcasted_iota(jnp.int32, (slot, cols), 1)
    half = lax.broadcasted_iota(jnp.int32, (slot, 128), 1)
    first_lanes = (lane % DH) < DH // 2
    first_half = (half % DH) < DH // 2
    ones_row = jnp.where(row1 == 10, 1.0, 0.0).astype(BF16)

    def segment(at):
        return seg_ref[at] - (blk * 2 * Z + 2 * at)

    def turn(a, query):
        other = jnp.where(first_lanes, pltpu.roll(a, cols - DH // 2, 1), pltpu.roll(a, DH // 2, 1))
        cosine = jnp.concatenate([cosv[query]] * pairs, axis=1)
        sine = jnp.concatenate([sinv[query]] * pairs, axis=1)
        return a * cosine + other * sine

    loads[0].wait()
    loads[1].wait()

    def project_q(query):
        at = order[query]
        seg = segment(at)
        length = qlen[query].astype(F32)
        count = jnp.sum(jnp.where(seg == 0, 1.0, 0.0), axis=1, keepdims=True)
        base0 = freq_ref[...] * length
        base1 = freq_ref[...] * (length - count)
        second = features(marks(var_ref[at], 1.0, seg), ones_row).astype(F32) > 0.5
        cos_a = jnp.where(second, jnp.cos(base1), jnp.cos(base0))
        sin_a = jnp.where(second, jnp.sin(base1), jnp.sin(base0))
        cosv[query] = cos_a * tcos_ref[...] - sin_a * tsin_ref[...]
        sine = sin_a * tcos_ref[...] + cos_a * tsin_ref[...]
        sinv[query] = jnp.where(first_half, -sine, sine)
        a = jnp.dot(xv[at], wq[...], preferred_element_type=F32)
        qrot[query] = (turn(a, query) * 0.125).astype(BF16)
        dv[query] = var_ref[at]

    each(Z, 0, project_q)

    pltpu.make_async_copy(ck.at[y], abuf.at[w], here.at[0]).wait()
    own_var.wait()

    def wait_a(i):
        src = (w + i) % W
        remote(abuf.at[src], abuf.at[src], s_a.at[src], r_a.at[src], y=src // C, c=src % C).wait_recv()
        remote(va.at[src], va.at[src], s_va.at[src], r_va.at[src], y=src // C, c=src % C).wait_recv()

    each(W, 1, wait_a)

    def line_b(to, at):
        return (remote(abuf.at[:, to], bbuf.at[pl.ds(at * W, W)], s_b.at[to], r_b.at[at], z=to),
                remote(va, vb.at[pl.ds(at * W, W)], s_vb.at[to], r_vb.at[at], z=to))

    def send_b(i):
        for copy in line_b((z + nth_near(i, Z)) % Z, z):
            copy.start()

    each(Z, 1, send_b)
    own_b = pltpu.make_async_copy(abuf.at[:, z], bbuf.at[pl.ds(z * W, W)], here.at[2])
    own_vb = pltpu.make_async_copy(va, vb.at[pl.ds(z * W, W)], here.at[3])
    own_b.start()
    own_vb.start()

    loads[2].wait()
    loads[3].wait()
    wide8 = lax.broadcasted_iota(jnp.int32, (8, cols), 1)
    deep8 = lax.broadcasted_iota(jnp.int32, (8, cols), 0)
    widen = jnp.where(wide8 // DH == deep8, 1.0, 0.0).astype(F32)

    def own_part(query):
        at = order[query]
        xs = xv[at]
        k = turn(jnp.dot(xs, wk[...], preferred_element_type=F32), query).astype(BF16)
        v = jnp.dot(xs, wv[...], preferred_element_type=F32).astype(BF16)
        seg = segment(at)
        qf = features(marks(var_ref[at], 1.0, seg), qtab[...])
        kf = features(marks(var_ref[at], 0.0, seg), ktab[...])
        q = qrot[query]
        stats = jnp.zeros((slot, 128), F32)
        for pair in range(pairs):
            tile = slice(pair * 128, pair * 128 + 128)
            outs = []
            for odd in range(2):
                mine = (half >= DH) if odd else (half < DH)
                qs = jnp.where(mine, q[:, tile], qf[:, tile])
                ks = jnp.where(mine, k[:, tile], kf)
                s = lax.dot_general(qs, ks, (((1,), (1,)), ((), ())), preferred_element_type=F32)
                m = jnp.max(s, axis=1, keepdims=True)
                p = jnp.exp(s - m)
                l = jnp.sum(p, axis=1, keepdims=True)
                outs.append(jnp.dot(p.astype(BF16), v[:, tile], preferred_element_type=F32) / l)
                head = 2 * pair + odd
                stats = jnp.where(half == head, m, jnp.where(half == 4 + head, l, stats))
            os[query, :, tile] = jnp.where(half < DH, outs[0], outs[1])
        sts[query] = jnp.transpose(stats)[:8]

    each(Z, 0, own_part)

    own_b.wait()
    own_vb.wait()

    def wait_b(i):
        src = (z + i) % Z
        part = bbuf.at[pl.ds(src * W, W)]
        remote(part, part, s_b.at[src], r_b.at[src], z=src).wait_recv()
        part = vb.at[pl.ds(src * W, W)]
        remote(part, part, s_vb.at[src], r_vb.at[src], z=src).wait_recv()

    each(Z, 1, wait_b)

    def pick(i):
        gbuf[i] = bbuf[inv[i]]

    each(Z * bpq, 0, pick)

    def line_g(to, at):
        return remote(gbuf.at[pl.ds(to * bpq, bpq)], kv.at[c, y, :, at], s_g.at[to], r_g.at[at], z=to)

    own_g = pltpu.make_async_copy(gbuf.at[pl.ds(z * bpq, bpq)], kv.at[c, y, :, z], here.at[2])
    own_g.start()
    each(Z, 1, lambda i: line_g((z + nth_near(i, Z)) % Z, z).start())

    def line_q(to, at):
        return (remote(qrot.at[to], qh.at[at], s_q.at[to], r_q.at[at], z=to),
                remote(dv.at[to], hv.at[at], s_dv.at[to], r_dv.at[at], z=to))

    def send_q(i):
        for copy in line_q((z + nth_near(i, Z)) % Z, z):
            copy.start()

    each(Z, 1, send_q)
    own_q = pltpu.make_async_copy(qrot.at[z], qh.at[z], here.at[0])
    own_dv = pltpu.make_async_copy(dv.at[z], hv.at[z], here.at[1])
    own_q.start()
    own_dv.start()
    own_g.wait()

    right, left, far, twin = (y + 1) % Y, (y + Y - 1) % Y, (y + 2) % Y, 1 - c

    def ring(kind, piece, at, send, recv, **device):
        part = kv.at[kind, piece, :, at]
        return remote(part, part, send.at[at], recv.at[at], **device)

    def to_twin(piece, at):
        return ring(c, piece, at, s_s.at[piece], r_s.at[piece], c=twin)

    def from_twin(piece, at):
        return ring(twin, piece, at, s_s.at[piece], r_s.at[piece], c=twin)

    to_right = lambda at: ring(c, y, at, s_r, r_l, y=right)
    to_left = lambda at: ring(c, y, at, s_l, r_r, y=left)
    from_left = lambda at: ring(c, left, at, s_r, r_l, y=left)
    from_right = lambda at: ring(c, right, at, s_l, r_r, y=right)
    pass_right = lambda at: ring(c, left, at, s_fr, r_fl, y=right)
    pass_left = lambda at: ring(c, right, at, s_fl, r_fr, y=left)
    far_left = lambda at: ring(c, far, at, s_fr, r_fl, y=left)
    far_right = lambda at: ring(c, far, at, s_fl, r_fr, y=right)

    def share(at):
        to_right(at).start()
        to_left(at).start()
        to_twin(y, at).start()

    def step1(i):
        at = (z + nth_near(i, Z)) % Z
        part = kv.at[c, y, :, at]
        remote(part, part, s_g.at[at], r_g.at[at], z=at).wait_recv()
        share(at)

    def step2(i):
        at = (z + nth_near(i, Z)) % Z
        from_left(at).wait_recv()

        @pl.when(at % 2 == 0)
        def _():
            pass_right(at).start()

        to_twin(left, at).start()
        from_right(at).wait_recv()

        @pl.when(at % 2 == 1)
        def _():
            pass_left(at).start()

        to_twin(right, at).start()

    def step3(i):
        at = (z + nth_near(i, Z)) % Z

        @pl.when(at % 2 == 0)
        def _():
            far_left(at).wait_recv()

        @pl.when(at % 2 == 1)
        def _():
            far_right(at).wait_recv()

        to_twin(far, at).start()

    share(z)
    each(Z, 1, step1)

    my_len = qlen[z]

    def build(n, piece):
        def one(j):
            var = vb[inv[z * bpq + j], piece]
            place = lane1 + (j * Y * slot + piece * slot)
            kf = features(marks(var, jnp.where(place >= my_len, 1.0, 0.0), None), ktab[...])
            k = kv[0, piece, j].reshape(slot, cols)
            v = kv[1, piece, j].reshape(slot, cols)
            rows = pl.ds(pl.multiple_of(j * slot, slot), slot)
            for pair in range(pairs):
                tile = slice(pair * 128, pair * 128 + 128)
                for odd in range(2):
                    mine = (half >= DH) if odd else (half < DH)
                    ka[2 * pair + odd, n, rows, :] = jnp.where(mine, k[:, tile], kf)
                    vx[2 * pair + odd, n, rows, :] = jnp.where(mine, v[:, tile], jnp.ones_like(kf))

        each(bpq, 0, one)

    def take_q(i):
        at = (z + nth_near(i, Z)) % Z
        qf = features(marks(hv[at], 1.0, None), qtab[...])
        q = qh[at]
        rows = pl.ds(pl.multiple_of(i * slot, slot), slot)
        for pair in range(pairs):
            tile = slice(pair * 128, pair * 128 + 128)
            for odd in range(2):
                mine = (half >= DH) if odd else (half < DH)
                qa[2 * pair + odd, rows, :] = jnp.where(mine, q[:, tile], qf[:, tile])

    def wait_q(i):
        at = (z + nth_near(i, Z)) % Z
        for copy in line_q(at, at):
            copy.wait_recv()
        take_q(i)

    side = Z // 2 * slot
    chunk = 256

    def attend(n, group, start):
        rows = slice(group * side, group * side + side)

        def one(h):
            q = qa[h, rows, :]
            if start:
                m = jnp.full((side, 128), -3e38, F32)[:, :1]
                total = None
            else:
                m = mx[h, rows, :][:, :1]
                total = acc[h, rows, :]
            for first in range(0, part_keys, chunk):
                s = lax.dot_general(q, ka[h, n, first:first + chunk, :], (((1,), (1,)), ((), ())),
                                    preferred_element_type=F32)
                new = jnp.maximum(m, jnp.max(s, axis=1, keepdims=True))
                p = jnp.exp(s - new).astype(BF16)
                o = jnp.dot(p, vx[h, n, first:first + chunk, :], preferred_element_type=F32)
                total = o if total is None else total * jnp.exp(m - new) + o
                m = new
            acc[h, rows, :] = total
            mx[h, rows, :] = jnp.broadcast_to(m, (side, 128))

        each(heads, 0, one)

    def twins(piece):
        each(Z, 0, lambda at: from_twin(piece, at).wait_recv())

    twins(y)
    build(0, y)
    own_q.wait()
    own_dv.wait()
    take_q(0)
    each(Z // 2, 1, wait_q)
    attend(0, 0, True)
    each(Z, 0, step2)
    each(Z, Z // 2, wait_q)
    attend(0, 1, True)
    each(Z, 0, step3)
    twins(left)
    build(1, left)
    twins(right)
    build(2, right)
    twins(far)
    build(3, far)

    def line_o(to, at):
        return (remote(oh.at[to], ro.at[at], s_o.at[to], r_o.at[at], z=to),
                remote(sth.at[to], rst.at[at], s_t.at[to], r_t.at[at], z=to))

    def settle(i):
        at = (z + nth_near(i, Z)) % Z
        rows = pl.ds(pl.multiple_of(i * slot, slot), slot)
        stats = jnp.zeros((slot, 128), F32)
        for pair in range(pairs):
            outs = []
            for odd in range(2):
                mine = (half >= DH) if odd else (half < DH)
                head = 2 * pair + odd
                total = acc[head, rows, :]
                turned = pltpu.roll(total, DH, 1)
                l = jnp.where(mine, turned, total)
                outs.append(total / l)
                stats = jnp.where(half == head, mx[head, rows, :], jnp.where(half == 4 + head, l, stats))
            oh[at, :, pair * 128:pair * 128 + 128] = jnp.where(half < DH, outs[0], outs[1]).astype(BF16)
        sth[at] = jnp.transpose(stats)[:8]

    def settle_send(i):
        settle(i)
        at = (z + nth_near(i, Z)) % Z
        for copy in line_o(at, z):
            copy.start()

    xright, xleft, xfar = (x + 1) % X, (x + X - 1) % X, (x + 2) % X
    mid_row = slot // 2
    keep = lambda at: pltpu.make_async_copy(att.at[at], attg.at[x, at], mine_sem.at[at])

    def xring(src, who, at, send, recv, dev):
        return remote(src, attg.at[who, at], send.at[at], recv.at[at], x=dev)

    def xpass(who, at, piece, send, recv, dev):
        part = attg.at[who, at, pl.ds(piece * mid_row, mid_row)]
        return remote(part, part, send.at[at], recv.at[at], x=dev)

    xto_right = lambda at: xring(att.at[at], x, at, x_r, y_l, xright)
    xto_left = lambda at: xring(att.at[at], x, at, x_l, y_r, xleft)
    xfrom_left = lambda at: xring(att.at[at], xleft, at, x_r, y_l, xleft)
    xfrom_right = lambda at: xring(att.at[at], xright, at, x_l, y_r, xright)
    xpass_right = lambda at: xpass(xleft, at, 0, x_fr, y_fl, xright)
    xpass_left = lambda at: xpass(xright, at, 1, x_fl, y_fr, xleft)
    xfar_left = lambda at: xpass(xfar, at, 0, x_fr, y_fl, xleft)
    xfar_right = lambda at: xpass(xfar, at, 1, x_fl, y_fr, xright)

    def join(at):
        far_m, far_l = rst[at][0:4], rst[at][4:8]
        own_m, own_l = sts[at][0:4], sts[at][4:8]
        m = jnp.maximum(far_m, own_m)
        a = far_l * jnp.exp(far_m - m)
        b = own_l * jnp.exp(own_m - m)
        total = a + b
        zero = jnp.zeros_like(total)

        def wide(share):
            return lax.dot_general(
                jnp.concatenate([share, zero], axis=0), widen, (((0,), (0,)), ((), ())),
                preferred_element_type=F32, precision=lax.Precision.HIGHEST)

        value = wide(a / total) * ro[at].astype(F32) + wide(b / total) * os[at]
        att[at] = value.astype(BF16)
        keep(at).start()
        xto_right(at).start()
        xto_left(at).start()

    def home(i):
        return (z + Z - nth_near(i, Z)) % Z

    def arrive(i):
        at = home(i)
        for copy in line_o(at, at):
            copy.wait_recv()
        join(at)

    def forward(i):
        at = home(i)
        xfrom_left(at).wait_recv()
        xpass_right(at).start()
        xfrom_right(at).wait_recv()
        xpass_left(at).start()

    for n in range(1, Y):
        attend(n, 0, False)
    settle(0)
    own_o = pltpu.make_async_copy(oh.at[z], ro.at[z], here.at[0])
    own_t = pltpu.make_async_copy(sth.at[z], rst.at[z], here.at[1])
    own_o.start()
    own_t.start()
    each(Z // 2, 1, settle_send)
    attend(1, 1, False)
    own_o.wait()
    own_t.wait()
    join(z)
    attend(2, 1, False)
    each(Z // 2, 1, arrive)
    attend(3, 1, False)
    each(Z, Z // 2, settle_send)
    each(Z // 2, 0, forward)

    def late(i):
        arrive(i)

        @pl.when(i > Z // 2)
        def _():
            forward(i - 1)

    each(Z, Z // 2, late)
    forward(Z - 1)

    def finish(at):
        xfar_left(at).wait_recv()
        xfar_right(at).wait_recv()
        keep(at).wait()
        for copy in (xto_right(at), xto_left(at), xpass_right(at), xpass_left(at), to_right(at), to_left(at)):
            copy.wait_send()

        @pl.when(at % 2 == 0)
        def _():
            pass_right(at).wait_send()

        @pl.when(at % 2 == 1)
        def _():
            pass_left(at).wait_send()

        for piece in range(Y):
            to_twin(piece, at).wait_send()

    each(Z, 0, finish)

    def end_line(i):
        at = (z + i) % Z
        for copy in line_b(at, at) + line_q(at, at) + line_o(at, at) + (line_g(at, at),):
            copy.wait_send()

    each(Z, 1, end_line)

    def end_cluster(i):
        to = (w + i) % W
        remote(abuf.at[to], abuf.at[to], s_a.at[to], r_a.at[to], y=to // C, c=to % C).wait_send()
        remote(cvar, va.at[to], s_va.at[to], r_va.at[to], y=to // C, c=to % C).wait_send()

    each(W, 1, end_cluster)


def out_kernel(dq, ids, att_ref, w_ref, x_ref, seg_ref, gain_ref, read_ref, upd_ref, pool_ref, y_ref):
    step = pl.program_id(0)
    parts, cols = att_ref.shape[0], att_ref.shape[3]
    y = jnp.dot(att_ref[0, 0], w_ref[0:cols, :], preferred_element_type=F32)
    for p in range(1, parts):
        y += jnp.dot(att_ref[p, 0], w_ref[p * cols:(p + 1) * cols, :], preferred_element_type=F32)
    y_ref[...] = y
    upd_ref[...] = y_ref[:, pl.ds(pl.multiple_of(ids[1] * cols, cols), cols)]
    hidden = x_ref[...].astype(F32) + y
    square = jnp.sum(hidden * hidden, axis=1, keepdims=True)
    weighted = jnp.sum(hidden * (gain_ref[...] * read_ref[...]), axis=1, keepdims=True)
    score = weighted * lax.rsqrt(square / y.shape[1] + 1e-06)
    first = (ids[0] * pl.num_programs(0) + step) * 2
    row = lax.broadcasted_iota(jnp.int32, (8, score.shape[0]), 0)
    member = jnp.where((row < 2) & (seg_ref[0] - first == row), 1.0, 0.0)
    sums = jnp.dot(member, jnp.broadcast_to(score, (score.shape[0], 128)),
                   preferred_element_type=F32, precision=lax.Precision.HIGHEST)
    count = jnp.maximum(jnp.sum(member, axis=1, keepdims=True), 1.0)
    pool_ref[0] = sums / count


def body(sizes, doc_x, doc_seg, doc_query, doc_var, query_len, block_perm, cache_k, cache_v, cache_var,
         w_query, w_key, w_value, w_out, var_bias, norm_gain, readout):
    X, Y, Z, C = sizes
    W = Y * C
    tokens, cols = doc_x.shape[0], w_query.shape[1]
    features = doc_x.shape[1]
    heads = cols // DH
    slot = tokens // Z
    crows = cache_k.shape[0]
    blocks = Y * Z * C
    bpq = blocks // Z
    piece = crows // (Y * Z)
    part_keys = bpq * slot
    i32 = jnp.int32
    dma = pltpu.SemaphoreType.DMA

    w_all = lax.all_gather(w_out, "x", axis=0, tiled=True)

    at = jnp.arange(blocks, dtype=i32)
    place = (at // C % Z) * W + (at // (Z * C)) * C + at % C
    inv = jnp.sum(jnp.where(block_perm[None, :] == at[:, None], place[None, :], 0), axis=1)

    half_size = DH // 2
    frequency = 10000.0 ** (-np.arange(half_size) / half_size)
    frequency = np.tile(frequency.astype(np.float32), 128 // half_size)
    turns = np.arange(slot)[:, None] * frequency.astype(np.float64)[None, :]
    seg = doc_seg.reshape(Z, 1, slot)

    vm = lambda *shape: pltpu.VMEM(shape, BF16)
    vf = lambda *shape: pltpu.VMEM(shape, F32)
    vi = lambda *shape: pltpu.VMEM(shape, i32)
    smem = pl.BlockSpec(memory_space=pltpu.SMEM)
    vmem = pl.BlockSpec(memory_space=pltpu.VMEM)
    hbm = pl.BlockSpec(memory_space=ANY)
    attended = pl.pallas_call(
        functools.partial(attention_kernel, sizes),
        in_specs=[smem] * 4 + [vmem] * 5 + [hbm] * 7,
        out_specs=hbm,
        out_shape=jax.ShapeDtypeStruct((X, Z, slot, cols), BF16),
        scratch_shapes=[
            vm(Z, slot, features), vm(features, cols), vm(features, cols), vm(features, cols),
            pltpu.SMEM((Z,), i32),
            vm(W, Z, piece, cols), vm(Z * W, piece, cols), vm(Z * bpq, piece, cols),
            vi(W, Y, 1, slot), vi(Z * W, Y, 1, slot),
            vm(C, Y, bpq, Z, piece, cols),
            vm(Z, slot, cols), vm(Z, slot, cols), vi(Z, 1, slot), vi(Z, 1, slot),
            vf(Z, slot, 128), vf(Z, slot, 128), vm(16, cols), vm(16, 128),
            vf(Z, slot, cols), vf(Z, 8, slot),
            vm(heads, Y, part_keys, 128), vm(heads, Y, part_keys, 128), vm(heads, tokens, 128),
            vf(heads, tokens, 128), vf(heads, tokens, 128),
            vm(Z, slot, cols), vf(Z, 8, slot), vm(Z, slot, cols), vf(Z, 8, slot), vm(Z, slot, cols),
            dma((4,)),
        ] + [dma((W,))] * 4 + [dma((Z,))] * 10 + [dma((Z,))] * 8 + [dma((Y, Z))] * 2
        + [dma((Z,))] * 4 + [dma((Z,))] * 9 + [dma((4,))],
        compiler_params=pltpu.CompilerParams(
            collective_id=0, has_side_effects=True, vmem_limit_bytes=56 << 20),
        name="attention",
    )(inv, doc_query, query_len, var_bias, seg, doc_var.reshape(Z, 1, slot),
      jnp.asarray(np.cos(turns), F32), jnp.asarray(np.sin(turns), F32), jnp.asarray(frequency)[None, :],
      doc_x.reshape(Z, slot, features), w_query, w_key, w_value,
      cache_k.reshape(Y, Z, piece, cols), cache_v.reshape(Y, Z, piece, cols), cache_var.reshape(Y, 1, slot))

    full = lambda *shape: pl.BlockSpec(shape, lambda i, *_: (0,) * len(shape))
    ids = jnp.stack([lax.axis_index(BLK), lax.axis_index("x")]).astype(i32)
    update, pooled = pl.pallas_call(
        out_kernel,
        grid_spec=pltpu.PrefetchScalarGridSpec(
            num_scalar_prefetch=2,
            grid=(Z,),
            in_specs=[
                pl.BlockSpec((X, 1, slot, cols), lambda i, d, n: (0, d[n[0] * 2 * Z + 2 * i], 0, 0)),
                full(X * cols, features),
                pl.BlockSpec((slot, features), lambda i, d, n: (i, 0)),
                pl.BlockSpec((1, 1, slot), lambda i, d, n: (i, 0, 0)),
                full(1, features),
                full(1, features),
            ],
            out_specs=[
                pl.BlockSpec((slot, cols), lambda i, d, n: (i, 0)),
                pl.BlockSpec((1, 8, 128), lambda i, d, n: (i, 0, 0)),
            ],
            scratch_shapes=[pltpu.VMEM((slot, features), F32)],
        ),
        out_shape=[
            jax.ShapeDtypeStruct((tokens, cols), F32),
            jax.ShapeDtypeStruct((Z, 8, 128), F32),
        ],
        compiler_params=pltpu.CompilerParams(vmem_limit_bytes=32 << 20),
        name="out_part",
    )(doc_query, ids, attended, w_all, doc_x, seg, norm_gain.reshape(1, features), readout.reshape(1, features))
    return update, pooled[:, :2, 0].reshape(2 * Z)


def solution(mesh):
    heads = mesh.shape["head"]
    cores = 2
    across = 4
    along = mesh.shape["blk"] // (across * cores)
    sizes = (heads, across, along, cores)
    split = Mesh(mesh.devices.reshape(sizes), ("x", "y", "z", "c"))
    return jax.shard_map(
        functools.partial(body, sizes),
        mesh=split,
        in_specs=(
            P(BLK, None), P(BLK), P(), P(BLK), P(), P(),
            P(BLK, "x"), P(BLK, "x"), P(BLK),
            P(None, "x"), P(None, "x"), P(None, "x"), P("x", None), P(None, "x"),
            P(), P(),
        ),
        out_specs=(P(BLK, "x"), P(BLK)),
        check_vma=False,
    )
```

time: 649 us -> 200 us (0.31)
  waiting for transfers between devices: 357 us -> 0.68 us
  Pallas kernels: 0 us -> 179 us
  matrix products: 87.6 us -> 0 us
  local copies, waits for them, and re-layouts: 66.9 us -> 3.87 us
  other arithmetic: 56 us -> 1.4 us
  blocking collectives: 31.1 us -> 0 us
  starting transfers between devices: 29.7 us -> 0.04 us
    all_to_all x3 -> x0, waiting for transfers between devices: 260 us -> none  [the longest x1 171 us: body(): lax.all_to_all(sums, 'blk', split_axis=0, concat_axis=0, tiled=True)]
    pallas_call x0 -> x2, Pallas kernels: none -> 179 us  [the longest x1 172 us: body(): pl.pallas_call(functools.partial(attention_kernel, sizes), in_specs=[smem...]
    psum x1 -> x0, waiting for transfers between devices: 96.1 us -> none  [body(): whole_sum = lax.psum(partial_update, 'head')]
    dot_general x43 -> x0, matrix products: 87.6 us -> none  [the longest x16 39.2 us: one_block(): jnp.einsum('thd,rhd->htr', block_q, cache_keys, preferred_element_type=jn...]
    all_to_all x2 -> x0, blocking collectives: 31.1 us -> none  [the longest x1 16.1 us: body(): lax.all_to_all(totals, 'blk', split_axis=0, concat_axis=0, tiled=True)]
    all_to_all x3 -> x0, starting transfers between devices: 29.5 us -> none  [the longest x1 12.1 us: body(): lax.all_to_all(send_var, 'blk', split_axis=0, concat_axis=0, tiled=True)]
    reduce_sum x21 -> x1, other arithmetic: 28.2 us -> 1.32 us  [body(): jnp.sum(jnp.where(block_perm[None, :] == at[:, None], place[None, :], 0),...]
    dynamic_update_slice x48 -> x0, local copies, waits for them, and re-layouts: 16.9 us -> none  [cache_part(): maxima, totals, sums = lax.map(one_block, (flat_q, flat_var))]
  transfers between devices with their start and end apart: 4 -> 1, of which waited for: 3 -> 0; matrix products, arithmetic and copies ran while one was open for 4% -> 1% of each run, Pallas kernels for 0% -> 86%
where the time goes in v2:
time: 200 us
  Pallas kernels  179 us (90%)
  between operations  14.1 us (7%)
  local copies, waits for them, and re-layouts  3.87 us (2%)
    pallas_call x1, Pallas kernels, body(): pl.pallas_call(functools.partial(attention_kernel, sizes), in_specs=[smem...  172 us
    pallas_call x1, Pallas kernels, body(): pl.pallas_call(out_kernel, grid_spec=pltpu.PrefetchScalarGridSpec(num_sca...  7.46 us
  transfers between devices with their start and end apart: 1, of which 0 were waited for; matrix products, arithmetic and copies ran while one was open for 1% of the time, Pallas kernels for 86%

profile of v2, /device:TPU:8, one launch (start us, length us, event | category | flops | bytes accessed | tf_op | source)
XLA Modules:
  0.0 199.5 jit_solution(1230308820947252044)
XLA Ops:
  7.2 0.0 all-gather.2.cloned.1.call-start
  7.2 0.7 all-gather.2.cloned.1.call-update
  7.9 1.3 select_reduce_fusion.inv
  9.2 0.0 copy-start
  9.2 0.0 copy-start.3
  9.2 0.0 copy-start.4
  9.2 0.0 copy-start.5
  9.2 0.0 copy-start.6
  9.3 172.0 %attention.1.att_ref = bf16[4,8,128,256]{3,2,1,0:T(8,128)(2,1)} custom-call(s32[64]{0:T(128)} %select_reduce_fusion.inv, s32[1024]{0:T(1024)} %dq.3, s32[8]{0:T(128)} %qlen.1, f32[2,4]{1,0:T(2,128)} %bias.1, s32[8,1,128]{2,1,0:T(1,128)} %bitcast.11, s32[8,1,128]{2,1,0:T(1,128)} %bitcast.17, f32[128,128]{1,0:T(8,128)} %constant.81.clone.tcos_ref, ...), custom_call_target="tpu_custom_call" | custom-call | tf_op jit(solution)/shard_map/attention/pallas_call | solution.py:619
  181.2 0.1 pad_add_fusion.ids
  181.3 0.0 all-gather.2.cloned.1.call-done.w_ref
  181.3 0.0 copy-done
  181.3 0.0 copy-done.3
  181.3 0.0 copy-done.4
  181.3 0.0 copy-done.5
  181.3 0.0 copy-done.6
  181.3 0.0 copy-start.1
  181.3 1.6 copy-done.1
  182.9 0.0 copy-start.2
  182.9 1.6 copy-done.2
  184.5 7.5 %out_part.1 = (f32[1024,256]{1,0:T(8,128)}, f32[8,8,128]{2,1,0:T(8,128)S(1)}) custom-call(s32[1024]{0:T(1024)S(1)} %copy-done.3, s32[2]{0:T(128)S(1)} %pad_add_fusion.ids, bf16[4,8,128,256]{3,2,1,0:T(8,128)(2,1)S(1)} %copy-done.1, bf16[1024,1024]{1,0:T(8,128)(2,1)S(1)} %copy-done.2, bf16[1024,1024]{1,0:T(8,128)(2,1)S(1)} %copy-done, ...), custom_call_target="tpu_custom_call" | custom-call | tf_op jit(solution)/shard_map/out_part/pallas_call | solution.py:649
  192.0 0.1 slice_reduce_fusion
  192.1 0.6 reshape_squeeze.3
  (1 shorter events, 0.0 us)
Async XLA Ops:
  7.2 174.1 %all-gather.2.cloned.1.call-start = ((), (), s32[]{:S(2)}) async-start(), calls=%async_computation | async-start | bytes 2621440 | tf_op jit(solution)/shard_map/all_gather | solution.py:601
  9.2 172.1 %copy-start = (bf16[1024,1024]{1,0:T(8,128)(2,1)S(1)}, bf16[1024,1024]{1,0:T(8,128)(2,1)}, u32[]{:S(2)}) copy-start(bf16[1024,1024]{1,0:T(8,128)(2,1)} %x_ref.1) | copy-start | bytes 6291460
  9.2 172.1 %copy-start.3 = (s32[1024]{0:T(1024)S(1)}, s32[1024]{0:T(1024)}, u32[]{:S(2)}) copy-start(s32[1024]{0:T(1024)} %dq.3) | copy-start | bytes 12292
  9.2 172.1 %copy-start.4 = (s32[1024]{0:T(1024)S(1)}, s32[1024]{0:T(1024)}, u32[]{:S(2)}) copy-start(s32[1024]{0:T(1024)} %param.20) | copy-start | bytes 12292
  9.2 172.1 %copy-start.5 = (f32[1024]{0:T(1024)S(1)}, f32[1024]{0:T(1024)}, u32[]{:S(2)}) copy-start(f32[1024]{0:T(1024)} %param.33) | copy-start | bytes 12292
  9.2 172.1 %copy-start.6 = (f32[1024]{0:T(1024)S(1)}, f32[1024]{0:T(1024)}, u32[]{:S(2)}) copy-start(f32[1024]{0:T(1024)} %param.34) | copy-start | bytes 12292
  181.3 1.6 copy-start.1
  182.9 1.6 copy-start.2
Sparse Core Ops, SparseCore 0:
  9.8 36.2 all-gather.1

commit v3 on v2

--- a/solution.py
+++ b/solution.py
@@ -41,12 +41,12 @@
 
 def attention_kernel(
     sizes, inv, dq, qlen, bias, seg_ref, var_ref, tcos_ref, tsin_ref, freq_ref, x_in, wq_in, wk_in, wv_in,
-    ck, cv, cvar, attg,
+    ck, cv, cvar, w_in, attg, w_all,
     xv, wq, wk, wv, order, abuf, bbuf, gbuf, va, vb, kv, qrot, qh, dv, hv, cosv, sinv, qtab, ktab,
     os, sts, ka, vx, qa, acc, mx, oh, sth, ro, rst, att,
     s_x, s_a, r_a, s_va, r_va, s_b, r_b, s_vb, r_vb, s_g, r_g, s_q, r_q, s_dv, r_dv,
     s_r, s_l, r_l, r_r, s_fr, s_fl, r_fl, r_fr, s_s, r_s,
-    s_o, r_o, s_t, r_t, x_r, x_l, y_l, y_r, x_fr, x_fl, y_fl, y_fr, mine_sem, here,
+    s_o, r_o, s_t, r_t, x_r, x_l, y_l, y_r, x_fr, x_fl, y_fl, y_fr, mine_sem, here, w_sem,
 ):
     X, Y, Z, C = sizes
     x, y, z, c = lax.axis_index("x"), lax.axis_index("y"), lax.axis_index("z"), lax.axis_index("c")
@@ -130,6 +130,21 @@
 
     own_var = pltpu.make_async_copy(cvar, va.at[w], here.at[1])
     own_var.start()
+
+    xright, xleft, xfar = (x + 1) % X, (x + X - 1) % X, (x + 2) % X
+    w_half = w_in.shape[0] // 2
+    w_keep = pltpu.make_async_copy(w_in, w_all.at[x], w_sem.at[8])
+
+    def w_whole(who, send, recv, dev):
+        return remote(w_in, w_all.at[who], w_sem.at[send], w_sem.at[recv], x=dev)
+
+    def w_pass(who, piece, send, recv, dev):
+        part = w_all.at[who, pl.ds(piece * w_half, w_half)]
+        return remote(part, part, w_sem.at[send], w_sem.at[recv], x=dev)
+
+    w_keep.start()
+    w_whole(x, 0, 2, xright).start()
+    w_whole(x, 1, 3, xleft).start()
 
     lane = lax.broadcasted_iota(jnp.int32, (slot, cols), 1)
     half = lax.broadcasted_iota(jnp.int32, (slot, 128), 1)
@@ -226,6 +241,10 @@
         sts[query] = jnp.transpose(stats)[:8]
 
     each(Z, 0, own_part)
+    w_whole(xleft, 0, 2, xleft).wait_recv()
+    w_pass(xleft, 0, 4, 6, xright).start()
+    w_whole(xright, 1, 3, xright).wait_recv()
+    w_pass(xright, 1, 5, 7, xleft).start()
 
     own_b.wait()
     own_vb.wait()
@@ -329,7 +348,16 @@
         to_twin(far, at).start()
 
     share(z)
-    each(Z, 1, step1)
+
+    def steps12(i):
+        step1(i)
+
+        @pl.when(i > 2)
+        def _():
+            step2(i - 3)
+
+    each(Z, 1, steps12)
+    each(Z, Z - 3, step2)
 
     my_len = qlen[z]
 
@@ -363,57 +391,42 @@
 
     def wait_q(i):
         at = (z + nth_near(i, Z)) % Z
-        for copy in line_q(at, at):
-            copy.wait_recv()
+
+        @pl.when(i == 0)
+        def _():
+            own_q.wait()
+            own_dv.wait()
+
+        @pl.when(i > 0)
+        def _():
+            for copy in line_q(at, at):
+                copy.wait_recv()
+
         take_q(i)
 
     side = Z // 2 * slot
-    chunk = 256
-
-    def attend(n, group, start):
-        rows = slice(group * side, group * side + side)
-
-        def one(h):
-            q = qa[h, rows, :]
-            if start:
-                m = jnp.full((side, 128), -3e38, F32)[:, :1]
-                total = None
-            else:
-                m = mx[h, rows, :][:, :1]
-                total = acc[h, rows, :]
-            for first in range(0, part_keys, chunk):
-                s = lax.dot_general(q, ka[h, n, first:first + chunk, :], (((1,), (1,)), ((), ())),
-                                    preferred_element_type=F32)
-                new = jnp.maximum(m, jnp.max(s, axis=1, keepdims=True))
-                p = jnp.exp(s - new).astype(BF16)
-                o = jnp.dot(p, vx[h, n, first:first + chunk, :], preferred_element_type=F32)
-                total = o if total is None else total * jnp.exp(m - new) + o
-                m = new
-            acc[h, rows, :] = total
+
+    def attend(n, group):
+        rows = pl.ds(pl.multiple_of(group * side, side), side)
+
+        def score(h):
+            return lax.dot_general(qa[h, rows, :], ka[h, n], (((1,), (1,)), ((), ())), preferred_element_type=F32)
+
+        def weigh(h, s):
+            old = mx[h, rows, :][:, :1]
+            m = jnp.maximum(old, jnp.max(s, axis=1, keepdims=True))
+            o = jnp.dot(jnp.exp(s - m).astype(BF16), vx[h, n], preferred_element_type=F32)
+            acc[h, rows, :] = acc[h, rows, :] * jnp.exp(old - m) + o
             mx[h, rows, :] = jnp.broadcast_to(m, (side, 128))
 
-        each(heads, 0, one)
+        s = score(0)
+        for h in range(heads):
+            later = score(h + 1) if h + 1 < heads else None
+            weigh(h, s)
+            s = later
 
     def twins(piece):
         each(Z, 0, lambda at: from_twin(piece, at).wait_recv())
-
-    twins(y)
-    build(0, y)
-    own_q.wait()
-    own_dv.wait()
-    take_q(0)
-    each(Z // 2, 1, wait_q)
-    attend(0, 0, True)
-    each(Z, 0, step2)
-    each(Z, Z // 2, wait_q)
-    attend(0, 1, True)
-    each(Z, 0, step3)
-    twins(left)
-    build(1, left)
-    twins(right)
-    build(2, right)
-    twins(far)
-    build(3, far)
 
     def line_o(to, at):
         return (remote(oh.at[to], ro.at[at], s_o.at[to], r_o.at[at], z=to),
@@ -436,13 +449,23 @@
             oh[at, :, pair * 128:pair * 128 + 128] = jnp.where(half < DH, outs[0], outs[1]).astype(BF16)
         sth[at] = jnp.transpose(stats)[:8]
 
+    own_o = pltpu.make_async_copy(oh.at[z], ro.at[z], here.at[2])
+    own_t = pltpu.make_async_copy(sth.at[z], rst.at[z], here.at[3])
+
     def settle_send(i):
         settle(i)
         at = (z + nth_near(i, Z)) % Z
-        for copy in line_o(at, z):
-            copy.start()
-
-    xright, xleft, xfar = (x + 1) % X, (x + X - 1) % X, (x + 2) % X
+
+        @pl.when(i == 0)
+        def _():
+            own_o.start()
+            own_t.start()
+
+        @pl.when(i > 0)
+        def _():
+            for copy in line_o(at, z):
+                copy.start()
+
     mid_row = slot // 2
     keep = lambda at: pltpu.make_async_copy(att.at[at], attg.at[x, at], mine_sem.at[at])
 
@@ -487,8 +510,17 @@
 
     def arrive(i):
         at = home(i)
-        for copy in line_o(at, at):
-            copy.wait_recv()
+
+        @pl.when(i == 0)
+        def _():
+            own_o.wait()
+            own_t.wait()
+
+        @pl.when(i > 0)
+        def _():
+            for copy in line_o(at, at):
+                copy.wait_recv()
+
         join(at)
 
     def forward(i):
@@ -498,23 +530,50 @@
         xfrom_right(at).wait_recv()
         xpass_left(at).start()
 
-    for n in range(1, Y):
-        attend(n, 0, False)
-    settle(0)
-    own_o = pltpu.make_async_copy(oh.at[z], ro.at[z], here.at[0])
-    own_t = pltpu.make_async_copy(sth.at[z], rst.at[z], here.at[1])
-    own_o.start()
-    own_t.start()
-    each(Z // 2, 1, settle_send)
-    attend(1, 1, False)
-    own_o.wait()
-    own_t.wait()
-    join(z)
-    attend(2, 1, False)
-    each(Z // 2, 1, arrive)
-    attend(3, 1, False)
-    each(Z, Z // 2, settle_send)
-    each(Z // 2, 0, forward)
+    hz = Z // 2
+
+    def main(t):
+        group, n = t // Y, t % Y
+        piece = jnp.where(n == 0, y, jnp.where(n == 1, left, jnp.where(n == 2, right, far)))
+
+        @pl.when(n == 0)
+        def _():
+            rows = pl.ds(pl.multiple_of(group * side, side), side)
+            for h in range(heads):
+                acc[h, rows, :] = jnp.zeros((side, 128), F32)
+                mx[h, rows, :] = jnp.full((side, 128), -3e38, F32)
+            each(hz, 0, lambda i: wait_q(group * hz + i))
+
+        @pl.when(t == 2)
+        def _():
+            each(Z, 0, step3)
+
+        @pl.when(t < Y)
+        def _():
+            twins(piece)
+            build(n, piece)
+
+        attend(n, group)
+
+        @pl.when(t == Y - 1)
+        def _():
+            each(hz, 0, settle_send)
+
+        @pl.when(t == Y)
+        def _():
+            arrive(0)
+
+        @pl.when(t == Y + 1)
+        def _():
+            each(hz, 1, arrive)
+
+        @pl.when(t == Y + 2)
+        def _():
+            forward(0)
+
+    each(2 * Y, 0, main)
+    each(Z, hz, settle_send)
+    each(hz, 1, forward)
 
     def late(i):
         arrive(i)
@@ -545,6 +604,12 @@
             to_twin(piece, at).wait_send()
 
     each(Z, 0, finish)
+    w_keep.wait()
+    w_pass(xfar, 0, 4, 6, xleft).wait_recv()
+    w_pass(xfar, 1, 5, 7, xright).wait_recv()
+    for copy in (w_whole(x, 0, 2, xright), w_whole(x, 1, 3, xleft),
+                 w_pass(xleft, 0, 4, 6, xright), w_pass(xright, 1, 5, 7, xleft)):
+        copy.wait_send()
 
     def end_line(i):
         at = (z + i) % Z
@@ -561,25 +626,28 @@
     each(W, 1, end_cluster)
 
 
-def out_kernel(dq, ids, att_ref, w_ref, x_ref, seg_ref, gain_ref, read_ref, upd_ref, pool_ref, y_ref):
+def out_kernel(dq, ids, att_ref, next_ref, w_ref, x_ref, seg_ref, gain_ref, read_ref, upd_ref, pool_ref, y_ref):
     step = pl.program_id(0)
-    parts, cols = att_ref.shape[0], att_ref.shape[3]
-    y = jnp.dot(att_ref[0, 0], w_ref[0:cols, :], preferred_element_type=F32)
-    for p in range(1, parts):
-        y += jnp.dot(att_ref[p, 0], w_ref[p * cols:(p + 1) * cols, :], preferred_element_type=F32)
+    parts, slot, cols = att_ref.shape[0], att_ref.shape[2], att_ref.shape[3]
+    y = None
+    for p in range(parts):
+        rows = jnp.concatenate([att_ref[p, 0], next_ref[p, 0]], axis=0)
+        part = jnp.dot(rows, w_ref[p], preferred_element_type=F32)
+        y = part if y is None else y + part
     y_ref[...] = y
     upd_ref[...] = y_ref[:, pl.ds(pl.multiple_of(ids[1] * cols, cols), cols)]
     hidden = x_ref[...].astype(F32) + y
     square = jnp.sum(hidden * hidden, axis=1, keepdims=True)
     weighted = jnp.sum(hidden * (gain_ref[...] * read_ref[...]), axis=1, keepdims=True)
     score = weighted * lax.rsqrt(square / y.shape[1] + 1e-06)
-    first = (ids[0] * pl.num_programs(0) + step) * 2
-    row = lax.broadcasted_iota(jnp.int32, (8, score.shape[0]), 0)
-    member = jnp.where((row < 2) & (seg_ref[0] - first == row), 1.0, 0.0)
-    sums = jnp.dot(member, jnp.broadcast_to(score, (score.shape[0], 128)),
-                   preferred_element_type=F32, precision=lax.Precision.HIGHEST)
-    count = jnp.maximum(jnp.sum(member, axis=1, keepdims=True), 1.0)
-    pool_ref[0] = sums / count
+    row = lax.broadcasted_iota(jnp.int32, (8, slot), 0)
+    for n in range(2):
+        first = (ids[0] * pl.num_programs(0) * 2 + step * 2 + n) * 2
+        member = jnp.where((row < 2) & (seg_ref[n] - first == row), 1.0, 0.0)
+        own = jnp.broadcast_to(score[n * slot:n * slot + slot], (slot, 128))
+        sums = jnp.dot(member, own, preferred_element_type=F32, precision=lax.Precision.HIGHEST)
+        count = jnp.maximum(jnp.sum(member, axis=1, keepdims=True), 1.0)
+        pool_ref[n] = sums / count
 
 
 def body(sizes, doc_x, doc_seg, doc_query, doc_var, query_len, block_perm, cache_k, cache_v, cache_var,
@@ -598,8 +666,6 @@
     i32 = jnp.int32
     dma = pltpu.SemaphoreType.DMA
 
-    w_all = lax.all_gather(w_out, "x", axis=0, tiled=True)
-
     at = jnp.arange(blocks, dtype=i32)
     place = (at // C % Z) * W + (at // (Z * C)) * C + at % C
     inv = jnp.sum(jnp.where(block_perm[None, :] == at[:, None], place[None, :], 0), axis=1)
@@ -616,11 +682,14 @@
     smem = pl.BlockSpec(memory_space=pltpu.SMEM)
     vmem = pl.BlockSpec(memory_space=pltpu.VMEM)
     hbm = pl.BlockSpec(memory_space=ANY)
-    attended = pl.pallas_call(
+    attended, w_all = pl.pallas_call(
         functools.partial(attention_kernel, sizes),
-        in_specs=[smem] * 4 + [vmem] * 5 + [hbm] * 7,
-        out_specs=hbm,
-        out_shape=jax.ShapeDtypeStruct((X, Z, slot, cols), BF16),
+        in_specs=[smem] * 4 + [vmem] * 5 + [hbm] * 8,
+        out_specs=[hbm] * 2,
+        out_shape=[
+            jax.ShapeDtypeStruct((X, Z, slot, cols), BF16),
+            jax.ShapeDtypeStruct((X, cols, features), BF16),
+        ],
         scratch_shapes=[
             vm(Z, slot, features), vm(features, cols), vm(features, cols), vm(features, cols),
             pltpu.SMEM((Z,), i32),
@@ -635,14 +704,14 @@
             vm(Z, slot, cols), vf(Z, 8, slot), vm(Z, slot, cols), vf(Z, 8, slot), vm(Z, slot, cols),
             dma((4,)),
         ] + [dma((W,))] * 4 + [dma((Z,))] * 10 + [dma((Z,))] * 8 + [dma((Y, Z))] * 2
-        + [dma((Z,))] * 4 + [dma((Z,))] * 9 + [dma((4,))],
+        + [dma((Z,))] * 4 + [dma((Z,))] * 9 + [dma((4,)), dma((9,))],
         compiler_params=pltpu.CompilerParams(
             collective_id=0, has_side_effects=True, vmem_limit_bytes=56 << 20),
         name="attention",
     )(inv, doc_query, query_len, var_bias, seg, doc_var.reshape(Z, 1, slot),
       jnp.asarray(np.cos(turns), F32), jnp.asarray(np.sin(turns), F32), jnp.asarray(frequency)[None, :],
       doc_x.reshape(Z, slot, features), w_query, w_key, w_value,
-      cache_k.reshape(Y, Z, piece, cols), cache_v.reshape(Y, Z, piece, cols), cache_var.reshape(Y, 1, slot))
+      cache_k.reshape(Y, Z, piece, cols), cache_v.reshape(Y, Z, piece, cols), cache_var.reshape(Y, 1, slot), w_out)
 
     full = lambda *shape: pl.BlockSpec(shape, lambda i, *_: (0,) * len(shape))
     ids = jnp.stack([lax.axis_index(BLK), lax.axis_index("x")]).astype(i32)
@@ -650,28 +719,30 @@
         out_kernel,
         grid_spec=pltpu.PrefetchScalarGridSpec(
             num_scalar_prefetch=2,
-            grid=(Z,),
+            grid=(Z // 2,),
             in_specs=[
-                pl.BlockSpec((X, 1, slot, cols), lambda i, d, n: (0, d[n[0] * 2 * Z + 2 * i], 0, 0)),
-                full(X * cols, features),
-                pl.BlockSpec((slot, features), lambda i, d, n: (i, 0)),
-                pl.BlockSpec((1, 1, slot), lambda i, d, n: (i, 0, 0)),
+                pl.BlockSpec((X, 1, slot, cols), lambda i, d, n: (0, d[n[0] * 2 * Z + 4 * i], 0, 0)),
+                pl.BlockSpec((X, 1, slot, cols), lambda i, d, n: (0, d[n[0] * 2 * Z + 4 * i + 2], 0, 0)),
+                full(X, cols, features),
+                pl.BlockSpec((2 * slot, features), lambda i, d, n: (i, 0)),
+                pl.BlockSpec((2, 1, slot), lambda i, d, n: (i, 0, 0)),
                 full(1, features),
                 full(1, features),
             ],
             out_specs=[
-                pl.BlockSpec((slot, cols), lambda i, d, n: (i, 0)),
-                pl.BlockSpec((1, 8, 128), lambda i, d, n: (i, 0, 0)),
+                pl.BlockSpec((2 * slot, cols), lambda i, d, n: (i, 0)),
+                pl.BlockSpec((2, 8, 128), lambda i, d, n: (i, 0, 0)),
             ],
-            scratch_shapes=[pltpu.VMEM((slot, features), F32)],
+            scratch_shapes=[pltpu.VMEM((2 * slot, features), F32)],
         ),
         out_shape=[
             jax.ShapeDtypeStruct((tokens, cols), F32),
             jax.ShapeDtypeStruct((Z, 8, 128), F32),
         ],
-        compiler_params=pltpu.CompilerParams(vmem_limit_bytes=32 << 20),
+        compiler_params=pltpu.CompilerParams(vmem_limit_bytes=60 << 20),
         name="out_part",
-    )(doc_query, ids, attended, w_all, doc_x, seg, norm_gain.reshape(1, features), readout.reshape(1, features))
+    )(doc_query, ids, attended, attended, w_all, doc_x, seg, norm_gain.reshape(1, features),
+      readout.reshape(1, features))
     return update, pooled[:, :2, 0].reshape(2 * Z)
 
 

time: 200 us -> 133 us (0.67); the launches traced: 200 us -> 130 us
  Pallas kernels: 179 us -> 126 us
  between operations: 14.1 us -> 0.65 us
  local copies, waits for them, and re-layouts: 3.87 us -> 1.44 us
    pallas_call x1, Pallas kernels: 172 us -> 118 us  [body(): pl.pallas_call(functools.partial(attention_kernel, sizes), in_specs=[smem...]
    unnamed x14 -> x0, local copies, waits for them, and re-layouts: 3.19 us -> none
  transfers between devices with their start and end apart: 1 -> 0, of which waited for: 0 -> 0; matrix products, arithmetic and copies ran while one was open for 1% -> 0% of each run, Pallas kernels for 86% -> 0%
where the time goes in v3:
time: 133 us; the launch traced here: 130 us
  Pallas kernels  126 us (95%)
  other arithmetic  1.95 us (1%)
  local copies, waits for them, and re-layouts  1.44 us (1%)
    pallas_call x1, Pallas kernels, body(): pl.pallas_call(functools.partial(attention_kernel, sizes), in_specs=[smem...  118 us
    pallas_call x1, Pallas kernels, body(): pl.pallas_call(out_kernel, grid_spec=pltpu.PrefetchScalarGridSpec(num_sca...  7.79 us

profile of v3, /device:TPU:8, one launch (start us, length us, event | category | flops | bytes accessed | tf_op | source)
XLA Modules:
  0.0 130.3 jit_solution(3405954973300866131)
XLA Ops:
  0.6 0.7 pad_add_fusion.ids
  1.3 1.3 select_reduce_fusion.inv
  2.6 118.5 %attention.1 = (bf16[4,8,128,256]{3,2,1,0:T(8,128)(2,1)}, bf16[4,256,1024]{2,1,0:T(8,128)(2,1)}) custom-call(s32[64]{0:T(128)} %select_reduce_fusion.inv, s32[1024]{0:T(1024)} %dq.3, s32[8]{0:T(128)} %qlen.1, f32[2,4]{1,0:T(2,128)} %bias.1, s32[8,1,128]{2,1,0:T(1,128)} %bitcast.13, s32[8,1,128]{2,1,0:T(1,128)} %bitcast.15, ...), custom_call_target="tpu_custom_call" | custom-call | tf_op jit(solution)/shard_map/attention/pallas_call | solution.py:685
  121.1 7.8 %out_part.1 = (f32[1024,256]{1,0:T(8,128)}, f32[8,8,128]{2,1,0:T(8,128)}) custom-call(s32[1024]{0:T(1024)} %dq.3, s32[2]{0:T(128)} %pad_add_fusion.ids, bf16[4,8,128,256]{3,2,1,0:T(8,128)(2,1)} %get-tuple-element.6.att_ref.next_ref, bf16[4,8,128,256]{3,2,1,0:T(8,128)(2,1)} %get-tuple-element.6.att_ref.next_ref, ...), custom_call_target="tpu_custom_call" | custom-call | tf_op jit(solution)/shard_map/out_part/pallas_call | solution.py:718
  128.9 0.8 slice_reduce_fusion
  129.7 0.6 reshape_squeeze.3
  (1 shorter events, 0.0 us)

commit v4 on v3

--- a/solution.py
+++ b/solution.py
@@ -43,7 +43,7 @@
     sizes, inv, dq, qlen, bias, seg_ref, var_ref, tcos_ref, tsin_ref, freq_ref, x_in, wq_in, wk_in, wv_in,
     ck, cv, cvar, w_in, attg, w_all,
     xv, wq, wk, wv, order, abuf, bbuf, gbuf, va, vb, kv, qrot, qh, dv, hv, cosv, sinv, qtab, ktab,
-    os, sts, ka, vx, qa, acc, mx, oh, sth, ro, rst, att,
+    os, sts, kfs, qfs, ka, vx, qa, acc, mx, oh, sth, ro, rst, att,
     s_x, s_a, r_a, s_va, r_va, s_b, r_b, s_vb, r_vb, s_g, r_g, s_q, r_q, s_dv, r_dv,
     s_r, s_l, r_l, r_r, s_fr, s_fl, r_fl, r_fr, s_s, r_s,
     s_o, r_o, s_t, r_t, x_r, x_l, y_l, y_r, x_fr, x_fl, y_fl, y_fr, mine_sem, here, w_sem,
@@ -195,7 +195,8 @@
 
     def line_b(to, at):
         return (remote(abuf.at[:, to], bbuf.at[pl.ds(at * W, W)], s_b.at[to], r_b.at[at], z=to),
-                remote(va, vb.at[pl.ds(at * W, W)], s_vb.at[to], r_vb.at[at], z=to))
+                remote(va, vb.at[pl.ds(at * W, W)], s_vb.at[to], r_vb.at[at], z=to),
+                remote(dv.at[to], hv.at[at], s_dv.at[to], r_dv.at[at], z=to))
 
     def send_b(i):
         for copy in line_b((z + nth_near(i, Z)) % Z, z):
@@ -204,8 +205,10 @@
     each(Z, 1, send_b)
     own_b = pltpu.make_async_copy(abuf.at[:, z], bbuf.at[pl.ds(z * W, W)], here.at[2])
     own_vb = pltpu.make_async_copy(va, vb.at[pl.ds(z * W, W)], here.at[3])
+    own_dv = pltpu.make_async_copy(dv.at[z], hv.at[z], here.at[1])
     own_b.start()
     own_vb.start()
+    own_dv.start()
 
     loads[2].wait()
     loads[3].wait()
@@ -240,7 +243,8 @@
             os[query, :, tile] = jnp.where(half < DH, outs[0], outs[1])
         sts[query] = jnp.transpose(stats)[:8]
 
-    each(Z, 0, own_part)
+    early = Z - 2
+    each(early, 0, own_part)
     w_whole(xleft, 0, 2, xleft).wait_recv()
     w_pass(xleft, 0, 4, 6, xright).start()
     w_whole(xright, 1, 3, xright).wait_recv()
@@ -248,6 +252,7 @@
 
     own_b.wait()
     own_vb.wait()
+    own_dv.wait()
 
     def wait_b(i):
         src = (z + i) % Z
@@ -255,6 +260,7 @@
         remote(part, part, s_b.at[src], r_b.at[src], z=src).wait_recv()
         part = vb.at[pl.ds(src * W, W)]
         remote(part, part, s_vb.at[src], r_vb.at[src], z=src).wait_recv()
+        remote(hv.at[src], hv.at[src], s_dv.at[src], r_dv.at[src], z=src).wait_recv()
 
     each(Z, 1, wait_b)
 
@@ -271,18 +277,11 @@
     each(Z, 1, lambda i: line_g((z + nth_near(i, Z)) % Z, z).start())
 
     def line_q(to, at):
-        return (remote(qrot.at[to], qh.at[at], s_q.at[to], r_q.at[at], z=to),
-                remote(dv.at[to], hv.at[at], s_dv.at[to], r_dv.at[at], z=to))
-
-    def send_q(i):
-        for copy in line_q((z + nth_near(i, Z)) % Z, z):
-            copy.start()
-
-    each(Z, 1, send_q)
+        return remote(qrot.at[to], qh.at[at], s_q.at[to], r_q.at[at], z=to)
+
+    each(Z, 1, lambda i: line_q((z + nth_near(i, Z)) % Z, z).start())
     own_q = pltpu.make_async_copy(qrot.at[z], qh.at[z], here.at[0])
-    own_dv = pltpu.make_async_copy(dv.at[z], hv.at[z], here.at[1])
     own_q.start()
-    own_dv.start()
     own_g.wait()
 
     right, left, far, twin = (y + 1) % Y, (y + Y - 1) % Y, (y + 2) % Y, 1 - c
@@ -348,27 +347,45 @@
         to_twin(far, at).start()
 
     share(z)
+    my_len = qlen[z]
+
+    def key_marks(i):
+        piece, j = i // bpq, i % bpq
+        var = vb[inv[z * bpq + j], piece]
+        place = lane1 + (j * Y * slot + piece * slot)
+        rows = pl.ds(pl.multiple_of(j * slot, slot), slot)
+        kfs[piece, rows, :] = features(marks(var, jnp.where(place >= my_len, 1.0, 0.0), None), ktab[...])
+
+    def query_marks(at):
+        qfs[at] = features(marks(hv[at], 1.0, None), qtab[...])
 
     def steps12(i):
         step1(i)
 
+        @pl.when(i < 5)
+        def _():
+            each(bpq * i, bpq * (i - 1), key_marks)
+
+        @pl.when(i == 5)
+        def _():
+            each(Z, 0, query_marks)
+
+        @pl.when(i > 5)
+        def _():
+            own_part(early + i - 6)
+
         @pl.when(i > 2)
         def _():
             step2(i - 3)
 
     each(Z, 1, steps12)
-    each(Z, Z - 3, step2)
-
-    my_len = qlen[z]
 
     def build(n, piece):
         def one(j):
-            var = vb[inv[z * bpq + j], piece]
-            place = lane1 + (j * Y * slot + piece * slot)
-            kf = features(marks(var, jnp.where(place >= my_len, 1.0, 0.0), None), ktab[...])
             k = kv[0, piece, j].reshape(slot, cols)
             v = kv[1, piece, j].reshape(slot, cols)
             rows = pl.ds(pl.multiple_of(j * slot, slot), slot)
+            kf = kfs[piece, rows, :]
             for pair in range(pairs):
                 tile = slice(pair * 128, pair * 128 + 128)
                 for odd in range(2):
@@ -380,7 +397,7 @@
 
     def take_q(i):
         at = (z + nth_near(i, Z)) % Z
-        qf = features(marks(hv[at], 1.0, None), qtab[...])
+        qf = qfs[at]
         q = qh[at]
         rows = pl.ds(pl.multiple_of(i * slot, slot), slot)
         for pair in range(pairs):
@@ -395,12 +412,10 @@
         @pl.when(i == 0)
         def _():
             own_q.wait()
-            own_dv.wait()
 
         @pl.when(i > 0)
         def _():
-            for copy in line_q(at, at):
-                copy.wait_recv()
+            line_q(at, at).wait_recv()
 
         take_q(i)
 
@@ -544,7 +559,7 @@
                 mx[h, rows, :] = jnp.full((side, 128), -3e38, F32)
             each(hz, 0, lambda i: wait_q(group * hz + i))
 
-        @pl.when(t == 2)
+        @pl.when(t == Y - 1)
         def _():
             each(Z, 0, step3)
 
@@ -554,6 +569,10 @@
             build(n, piece)
 
         attend(n, group)
+
+        @pl.when(t == 0)
+        def _():
+            each(Z, Z - 3, step2)
 
         @pl.when(t == Y - 1)
         def _():
@@ -613,7 +632,7 @@
 
     def end_line(i):
         at = (z + i) % Z
-        for copy in line_b(at, at) + line_q(at, at) + line_o(at, at) + (line_g(at, at),):
+        for copy in line_b(at, at) + line_o(at, at) + (line_q(at, at), line_g(at, at)):
             copy.wait_send()
 
     each(Z, 1, end_line)
@@ -647,7 +666,9 @@
         own = jnp.broadcast_to(score[n * slot:n * slot + slot], (slot, 128))
         sums = jnp.dot(member, own, preferred_element_type=F32, precision=lax.Precision.HIGHEST)
         count = jnp.maximum(jnp.sum(member, axis=1, keepdims=True), 1.0)
-        pool_ref[n] = sums / count
+        mean = sums / count
+        for k in range(2):
+            pool_ref[step * 4 + n * 2 + k] = mean[k, 0]
 
 
 def body(sizes, doc_x, doc_seg, doc_query, doc_var, query_len, block_perm, cache_k, cache_v, cache_var,
@@ -698,7 +719,7 @@
             vm(C, Y, bpq, Z, piece, cols),
             vm(Z, slot, cols), vm(Z, slot, cols), vi(Z, 1, slot), vi(Z, 1, slot),
             vf(Z, slot, 128), vf(Z, slot, 128), vm(16, cols), vm(16, 128),
-            vf(Z, slot, cols), vf(Z, 8, slot),
+            vf(Z, slot, cols), vf(Z, 8, slot), vm(Y, part_keys, 128), vm(Z, slot, cols),
             vm(heads, Y, part_keys, 128), vm(heads, Y, part_keys, 128), vm(heads, tokens, 128),
             vf(heads, tokens, 128), vf(heads, tokens, 128),
             vm(Z, slot, cols), vf(Z, 8, slot), vm(Z, slot, cols), vf(Z, 8, slot), vm(Z, slot, cols),
@@ -731,19 +752,19 @@
             ],
             out_specs=[
                 pl.BlockSpec((2 * slot, cols), lambda i, d, n: (i, 0)),
-                pl.BlockSpec((2, 8, 128), lambda i, d, n: (i, 0, 0)),
+                smem,
             ],
             scratch_shapes=[pltpu.VMEM((2 * slot, features), F32)],
         ),
         out_shape=[
             jax.ShapeDtypeStruct((tokens, cols), F32),
-            jax.ShapeDtypeStruct((Z, 8, 128), F32),
+            jax.ShapeDtypeStruct((2 * Z,), F32),
         ],
         compiler_params=pltpu.CompilerParams(vmem_limit_bytes=60 << 20),
         name="out_part",
     )(doc_query, ids, attended, attended, w_all, doc_x, seg, norm_gain.reshape(1, features),
       readout.reshape(1, features))
-    return update, pooled[:, :2, 0].reshape(2 * Z)
+    return update, pooled
 
 
 def solution(mesh):

time: 133 us -> 130 us (0.977)
  the two profiles are of different devices: /device:TPU:8 before, /device:TPU:64 now
where the time goes in v4:
time: 130 us
  Pallas kernels  127 us (98%)
  other arithmetic  1.88 us (1%)
    pallas_call x1, Pallas kernels, body(): pl.pallas_call(functools.partial(attention_kernel, sizes), in_specs=[smem...  119 us
    pallas_call x1, Pallas kernels, body(): pl.pallas_call(out_kernel, grid_spec=pltpu.PrefetchScalarGridSpec(num_sca...  7.97 us

profile of v4, /device:TPU:64, one launch (start us, length us, event | category | flops | bytes accessed | tf_op | source)
XLA Modules:
  0.0 129.5 jit_solution(5166081922049106563)
XLA Ops:
  0.6 0.6 pad_add_fusion.ids
  1.2 1.3 select_reduce_fusion.inv
  2.5 119.0 %attention.1 = (bf16[4,8,128,256]{3,2,1,0:T(8,128)(2,1)}, bf16[4,256,1024]{2,1,0:T(8,128)(2,1)}) custom-call(s32[64]{0:T(128)} %select_reduce_fusion.inv, s32[1024]{0:T(1024)} %dq.3, s32[8]{0:T(128)} %qlen.1, f32[2,4]{1,0:T(2,128)} %bias.1, s32[8,1,128]{2,1,0:T(1,128)} %bitcast.13, s32[8,1,128]{2,1,0:T(1,128)} %bitcast.15, ...), custom_call_target="tpu_custom_call" | custom-call | tf_op jit(solution)/shard_map/attention/pallas_call | solution.py:706
  121.6 8.0 %out_part.1 = (f32[1024,256]{1,0:T(8,128)}, f32[16]{0:T(128)}) custom-call(s32[1024]{0:T(1024)} %dq.3, s32[2]{0:T(128)} %pad_add_fusion.ids, bf16[4,8,128,256]{3,2,1,0:T(8,128)(2,1)} %get-tuple-element.4.att_ref.next_ref, bf16[4,8,128,256]{3,2,1,0:T(8,128)(2,1)} %get-tuple-element.4.att_ref.next_ref, bf16[4,256,1024]{2,1,0:T(8,128)(2,1)} %get-tuple-element.5.w_ref, ...), custom_call_target="tpu_custom_call" | custom-call | tf_op jit(solution)/shard_map/out_part/pallas_call | solution.py:739
  (1 shorter events, 0.0 us)

commit v5 on v4

--- a/solution.py
+++ b/solution.py
@@ -40,9 +40,9 @@
 
 
 def attention_kernel(
-    sizes, inv, dq, qlen, bias, seg_ref, var_ref, tcos_ref, tsin_ref, freq_ref, x_in, wq_in, wk_in, wv_in,
-    ck, cv, cvar, w_in, attg, w_all,
-    xv, wq, wk, wv, order, abuf, bbuf, gbuf, va, vb, kv, qrot, qh, dv, hv, cosv, sinv, qtab, ktab,
+    sizes, perm, dq, qlen, bias, seg_ref, var_ref, tcos_ref, tsin_ref, freq_ref, x_in, wq_in, wk_in, wv_in,
+    ck, cv, cvar, w_in, attg, w_all, ids,
+    inv, xv, wq, wk, wv, order, abuf, bbuf, gbuf, va, vb, kv, qrot, qh, dv, hv, cosv, sinv, qtab, ktab,
     os, sts, kfs, qfs, ka, vx, qa, acc, mx, oh, sth, ro, rst, att,
     s_x, s_a, r_a, s_va, r_va, s_b, r_b, s_vb, r_vb, s_g, r_g, s_q, r_q, s_dv, r_dv,
     s_r, s_l, r_l, r_r, s_fr, s_fl, r_fl, r_fr, s_s, r_s,
@@ -182,6 +182,16 @@
         dv[query] = var_ref[at]
 
     each(Z, 0, project_q)
+
+    def line_q(to, at):
+        return remote(qrot.at[to], qh.at[at], s_q.at[to], r_q.at[at], z=to)
+
+    def send_q(i):
+        line_q((z + nth_near(i, Z)) % Z, z).start()
+
+    each(Z // 2, 1, send_q)
+    own_q = pltpu.make_async_copy(qrot.at[z], qh.at[z], here.at[4])
+    own_q.start()
 
     pltpu.make_async_copy(ck.at[y], abuf.at[w], here.at[0]).wait()
     own_var.wait()
@@ -243,8 +253,18 @@
             os[query, :, tile] = jnp.where(half < DH, outs[0], outs[1])
         sts[query] = jnp.transpose(stats)[:8]
 
-    early = Z - 2
+    early = Z // 2 - 1
     each(early, 0, own_part)
+
+    def find(k):
+        at = jnp.int32(0)
+        for e in range(Z * W):
+            at = jnp.where(perm[e] == k, e // C % Z * W + e // (Z * C) * C + e % C, at)
+        inv[k] = at
+
+    each(Z * W, 0, find)
+    ids[0] = blk
+    ids[1] = x
     w_whole(xleft, 0, 2, xleft).wait_recv()
     w_pass(xleft, 0, 4, 6, xright).start()
     w_whole(xright, 1, 3, xright).wait_recv()
@@ -276,12 +296,7 @@
     own_g.start()
     each(Z, 1, lambda i: line_g((z + nth_near(i, Z)) % Z, z).start())
 
-    def line_q(to, at):
-        return remote(qrot.at[to], qh.at[at], s_q.at[to], r_q.at[at], z=to)
-
-    each(Z, 1, lambda i: line_q((z + nth_near(i, Z)) % Z, z).start())
-    own_q = pltpu.make_async_copy(qrot.at[z], qh.at[z], here.at[0])
-    own_q.start()
+    each(Z, Z // 2, send_q)
     own_g.wait()
 
     right, left, far, twin = (y + 1) % Y, (y + Y - 1) % Y, (y + 2) % Y, 1 - c
@@ -362,17 +377,14 @@
     def steps12(i):
         step1(i)
 
-        @pl.when(i < 5)
-        def _():
-            each(bpq * i, bpq * (i - 1), key_marks)
-
-        @pl.when(i == 5)
-        def _():
-            each(Z, 0, query_marks)
-
-        @pl.when(i > 5)
-        def _():
-            own_part(early + i - 6)
+        @pl.when(i < 3)
+        def _():
+            each(2 * bpq * i, 2 * bpq * (i - 1), key_marks)
+            each(Z // 2 * i, Z // 2 * (i - 1), query_marks)
+
+        @pl.when(i > 2)
+        def _():
+            own_part(early + i - 3)
 
         @pl.when(i > 2)
         def _():
@@ -506,15 +518,11 @@
         m = jnp.maximum(far_m, own_m)
         a = far_l * jnp.exp(far_m - m)
         b = own_l * jnp.exp(own_m - m)
-        total = a + b
-        zero = jnp.zeros_like(total)
-
-        def wide(share):
-            return lax.dot_general(
-                jnp.concatenate([share, zero], axis=0), widen, (((0,), (0,)), ((), ())),
-                preferred_element_type=F32, precision=lax.Precision.HIGHEST)
-
-        value = wide(a / total) * ro[at].astype(F32) + wide(b / total) * os[at]
+        share = a / (a + b)
+        wide = lax.dot_general(
+            jnp.concatenate([share, jnp.zeros_like(share)], axis=0), widen, (((0,), (0,)), ((), ())),
+            preferred_element_type=F32, precision=lax.Precision.HIGHEST)
+        value = os[at] + wide * (ro[at].astype(F32) - os[at])
         att[at] = value.astype(BF16)
         keep(at).start()
         xto_right(at).start()
@@ -687,10 +695,6 @@
     i32 = jnp.int32
     dma = pltpu.SemaphoreType.DMA
 
-    at = jnp.arange(blocks, dtype=i32)
-    place = (at // C % Z) * W + (at // (Z * C)) * C + at % C
-    inv = jnp.sum(jnp.where(block_perm[None, :] == at[:, None], place[None, :], 0), axis=1)
-
     half_size = DH // 2
     frequency = 10000.0 ** (-np.arange(half_size) / half_size)
     frequency = np.tile(frequency.astype(np.float32), 128 // half_size)
@@ -703,16 +707,17 @@
     smem = pl.BlockSpec(memory_space=pltpu.SMEM)
     vmem = pl.BlockSpec(memory_space=pltpu.VMEM)
     hbm = pl.BlockSpec(memory_space=ANY)
-    attended, w_all = pl.pallas_call(
+    attended, w_all, ids = pl.pallas_call(
         functools.partial(attention_kernel, sizes),
         in_specs=[smem] * 4 + [vmem] * 5 + [hbm] * 8,
-        out_specs=[hbm] * 2,
+        out_specs=[hbm] * 2 + [smem],
         out_shape=[
             jax.ShapeDtypeStruct((X, Z, slot, cols), BF16),
             jax.ShapeDtypeStruct((X, cols, features), BF16),
+            jax.ShapeDtypeStruct((2,), i32),
         ],
         scratch_shapes=[
-            vm(Z, slot, features), vm(features, cols), vm(features, cols), vm(features, cols),
+            pltpu.SMEM((blocks,), i32), vm(Z, slot, features), vm(features, cols), vm(features, cols), vm(features, cols),
             pltpu.SMEM((Z,), i32),
             vm(W, Z, piece, cols), vm(Z * W, piece, cols), vm(Z * bpq, piece, cols),
             vi(W, Y, 1, slot), vi(Z * W, Y, 1, slot),
@@ -725,17 +730,16 @@
             vm(Z, slot, cols), vf(Z, 8, slot), vm(Z, slot, cols), vf(Z, 8, slot), vm(Z, slot, cols),
             dma((4,)),
         ] + [dma((W,))] * 4 + [dma((Z,))] * 10 + [dma((Z,))] * 8 + [dma((Y, Z))] * 2
-        + [dma((Z,))] * 4 + [dma((Z,))] * 9 + [dma((4,)), dma((9,))],
+        + [dma((Z,))] * 4 + [dma((Z,))] * 9 + [dma((5,)), dma((9,))],
         compiler_params=pltpu.CompilerParams(
             collective_id=0, has_side_effects=True, vmem_limit_bytes=56 << 20),
         name="attention",
-    )(inv, doc_query, query_len, var_bias, seg, doc_var.reshape(Z, 1, slot),
+    )(block_perm, doc_query, query_len, var_bias, seg, doc_var.reshape(Z, 1, slot),
       jnp.asarray(np.cos(turns), F32), jnp.asarray(np.sin(turns), F32), jnp.asarray(frequency)[None, :],
       doc_x.reshape(Z, slot, features), w_query, w_key, w_value,
       cache_k.reshape(Y, Z, piece, cols), cache_v.reshape(Y, Z, piece, cols), cache_var.reshape(Y, 1, slot), w_out)
 
     full = lambda *shape: pl.BlockSpec(shape, lambda i, *_: (0,) * len(shape))
-    ids = jnp.stack([lax.axis_index(BLK), lax.axis_index("x")]).astype(i32)
     update, pooled = pl.pallas_call(
         out_kernel,
         grid_spec=pltpu.PrefetchScalarGridSpec(

time: 130 us -> 128 us (0.985)
  the two profiles are of different devices: /device:TPU:64 before, /device:TPU:8 now
where the time goes in v5:
time: 128 us; the launch traced here: 125 us
  Pallas kernels  125 us (98%)
    pallas_call x1, Pallas kernels, body(): pl.pallas_call(functools.partial(attention_kernel, sizes), in_specs=[smem...  117 us
    pallas_call x1, Pallas kernels, body(): pl.pallas_call(out_kernel, grid_spec=pltpu.PrefetchScalarGridSpec(num_sca...  7.97 us

profile of v5, /device:TPU:8, one launch (start us, length us, event | category | flops | bytes accessed | tf_op | source)
XLA Modules:
  0.0 125.3 jit_solution(6180048746171910788)
XLA Ops:
  0.6 116.7 %attention.1 = (bf16[4,8,128,256]{3,2,1,0:T(8,128)(2,1)}, bf16[4,256,1024]{2,1,0:T(8,128)(2,1)}, s32[2]{0:T(128)}) custom-call(s32[64]{0:T(128)} %perm.1, s32[1024]{0:T(1024)} %dq.3, s32[8]{0:T(128)} %qlen.1, f32[2,4]{1,0:T(2,128)} %bias.1, s32[8,1,128]{2,1,0:T(1,128)} %bitcast.11, s32[8,1,128]{2,1,0:T(1,128)} %bitcast.13, ...), custom_call_target="tpu_custom_call" | custom-call | tf_op jit(solution)/shard_map/attention/pallas_call | solution.py:710
  117.4 8.0 %out_part.1 = (f32[1024,256]{1,0:T(8,128)}, f32[16]{0:T(128)}) custom-call(s32[1024]{0:T(1024)} %dq.3, s32[2]{0:T(128)} %get-tuple-element.5.ids, bf16[4,8,128,256]{3,2,1,0:T(8,128)(2,1)} %get-tuple-element.6.att_ref.next_ref, bf16[4,8,128,256]{3,2,1,0:T(8,128)(2,1)} %get-tuple-element.6.att_ref.next_ref, bf16[4,256,1024]{2,1,0:T(8,128)(2,1)} %get-tuple-element.7.w_ref, ...), custom_call_target="tpu_custom_call" | custom-call | tf_op jit(solution)/shard_map/out_part/pallas_call | solution.py:743

commit v6 on v5

--- a/solution.py
+++ b/solution.py
@@ -567,20 +567,20 @@
                 mx[h, rows, :] = jnp.full((side, 128), -3e38, F32)
             each(hz, 0, lambda i: wait_q(group * hz + i))
 
-        @pl.when(t == Y - 1)
-        def _():
-            each(Z, 0, step3)
-
         @pl.when(t < Y)
         def _():
             twins(piece)
             build(n, piece)
 
+        @pl.when(t == 0)
+        def _():
+            each(Z, Z - 3, step2)
+
         attend(n, group)
 
-        @pl.when(t == 0)
-        def _():
-            each(Z, Z - 3, step2)
+        @pl.when(t == 1)
+        def _():
+            each(Z, 0, step3)
 
         @pl.when(t == Y - 1)
         def _():
@@ -656,11 +656,8 @@
 def out_kernel(dq, ids, att_ref, next_ref, w_ref, x_ref, seg_ref, gain_ref, read_ref, upd_ref, pool_ref, y_ref):
     step = pl.program_id(0)
     parts, slot, cols = att_ref.shape[0], att_ref.shape[2], att_ref.shape[3]
-    y = None
-    for p in range(parts):
-        rows = jnp.concatenate([att_ref[p, 0], next_ref[p, 0]], axis=0)
-        part = jnp.dot(rows, w_ref[p], preferred_element_type=F32)
-        y = part if y is None else y + part
+    rows = [jnp.concatenate([ref[p, 0] for p in range(parts)], axis=1) for ref in (att_ref, next_ref)]
+    y = jnp.dot(jnp.concatenate(rows, axis=0), w_ref[...], preferred_element_type=F32)
     y_ref[...] = y
     upd_ref[...] = y_ref[:, pl.ds(pl.multiple_of(ids[1] * cols, cols), cols)]
     hidden = x_ref[...].astype(F32) + y
@@ -748,7 +745,7 @@
             in_specs=[
                 pl.BlockSpec((X, 1, slot, cols), lambda i, d, n: (0, d[n[0] * 2 * Z + 4 * i], 0, 0)),
                 pl.BlockSpec((X, 1, slot, cols), lambda i, d, n: (0, d[n[0] * 2 * Z + 4 * i + 2], 0, 0)),
-                full(X, cols, features),
+                full(X * cols, features),
                 pl.BlockSpec((2 * slot, features), lambda i, d, n: (i, 0)),
                 pl.BlockSpec((2, 1, slot), lambda i, d, n: (i, 0, 0)),
                 full(1, features),
@@ -766,7 +763,7 @@
         ],
         compiler_params=pltpu.CompilerParams(vmem_limit_bytes=60 << 20),
         name="out_part",
-    )(doc_query, ids, attended, attended, w_all, doc_x, seg, norm_gain.reshape(1, features),
+    )(doc_query, ids, attended, attended, w_all.reshape(X * cols, features), doc_x, seg, norm_gain.reshape(1, features),
       readout.reshape(1, features))
     return update, pooled
 

time: 128 us -> 127 us (level); the launches traced: 125 us -> 126 us
  no operation moved by 1% of the time
where the time goes in v6:
time: 127 us; the launch traced here: 126 us
  Pallas kernels  125 us (98%)
    pallas_call x1, Pallas kernels, body(): pl.pallas_call(functools.partial(attention_kernel, sizes), in_specs=[smem...  117 us
    pallas_call x1, Pallas kernels, body(): pl.pallas_call(out_kernel, grid_spec=pltpu.PrefetchScalarGridSpec(num_sca...  8.03 us

profile of v6, /device:TPU:8, one launch (start us, length us, event | category | flops | bytes accessed | tf_op | source)
XLA Modules:
  0.0 125.8 jit_solution(4576276127306277219)
XLA Ops:
  0.6 117.1 %attention.1 = (bf16[4,8,128,256]{3,2,1,0:T(8,128)(2,1)}, bf16[4,256,1024]{2,1,0:T(8,128)(2,1)}, s32[2]{0:T(128)}) custom-call(s32[64]{0:T(128)} %perm.1, s32[1024]{0:T(1024)} %dq.3, s32[8]{0:T(128)} %qlen.1, f32[2,4]{1,0:T(2,128)} %bias.1, s32[8,1,128]{2,1,0:T(1,128)} %bitcast.13, s32[8,1,128]{2,1,0:T(1,128)} %bitcast.15, ...), custom_call_target="tpu_custom_call" | custom-call | tf_op jit(solution)/shard_map/attention/pallas_call | solution.py:707
  117.8 8.0 %out_part.1 = (f32[1024,256]{1,0:T(8,128)}, f32[16]{0:T(128)}) custom-call(s32[1024]{0:T(1024)} %dq.3, s32[2]{0:T(128)} %get-tuple-element.5.ids, bf16[4,8,128,256]{3,2,1,0:T(8,128)(2,1)} %get-tuple-element.6.att_ref.next_ref, bf16[4,8,128,256]{3,2,1,0:T(8,128)(2,1)} %get-tuple-element.6.att_ref.next_ref, bf16[1024,1024]{1,0:T(8,128)(2,1)} %bitcast.10, ...), custom_call_target="tpu_custom_call" | custom-call | tf_op jit(solution)/shard_map/out_part/pallas_call | solution.py:740

commit v7 on v6

--- a/solution.py
+++ b/solution.py
@@ -40,13 +40,12 @@
 
 
 def attention_kernel(
-    sizes, perm, dq, qlen, bias, seg_ref, var_ref, tcos_ref, tsin_ref, freq_ref, x_in, wq_in, wk_in, wv_in,
-    ck, cv, cvar, w_in, attg, w_all, ids,
-    inv, xv, wq, wk, wv, order, abuf, bbuf, gbuf, va, vb, kv, qrot, qh, dv, hv, cosv, sinv, qtab, ktab,
-    os, sts, kfs, qfs, ka, vx, qa, acc, mx, oh, sth, ro, rst, att,
+    sizes, perm, dq, qlen, bias, seg_ref, var_ref, tcos_ref, tsin_ref, freq_ref, x_in, wq_in, wk_in, wv_in, gain_ref, read_ref, ck, cv, cvar, w_in, upd, pool,
+    attg, w_all, ytmp, yown, yout, means, inv, xv, wq, wk, wv, order, abuf, bbuf, gbuf, va, vb, kv, qrot, qh, dv, hv, cosv, sinv, qtab, ktab,
+    os, sts, kfs, qfs, ka, vx, qa, acc, mx, oh, sth, ro, rst,
     s_x, s_a, r_a, s_va, r_va, s_b, r_b, s_vb, r_vb, s_g, r_g, s_q, r_q, s_dv, r_dv,
     s_r, s_l, r_l, r_r, s_fr, s_fl, r_fl, r_fr, s_s, r_s,
-    s_o, r_o, s_t, r_t, x_r, x_l, y_l, y_r, x_fr, x_fl, y_fl, y_fr, mine_sem, here, w_sem,
+    s_o, r_o, s_t, r_t, x_r, x_l, y_l, y_r, x_fr, x_fl, y_fl, y_fr, here, w_sem, out_sem,
 ):
     X, Y, Z, C = sizes
     x, y, z, c = lax.axis_index("x"), lax.axis_index("y"), lax.axis_index("z"), lax.axis_index("c")
@@ -263,8 +262,6 @@
         inv[k] = at
 
     each(Z * W, 0, find)
-    ids[0] = blk
-    ids[1] = x
     w_whole(xleft, 0, 2, xleft).wait_recv()
     w_pass(xleft, 0, 4, 6, xright).start()
     w_whole(xright, 1, 3, xright).wait_recv()
@@ -494,19 +491,19 @@
                 copy.start()
 
     mid_row = slot // 2
-    keep = lambda at: pltpu.make_async_copy(att.at[at], attg.at[x, at], mine_sem.at[at])
-
-    def xring(src, who, at, send, recv, dev):
-        return remote(src, attg.at[who, at], send.at[at], recv.at[at], x=dev)
+
+    def xring(who, at, send, recv, dev):
+        part = attg.at[who, at]
+        return remote(part, part, send.at[at], recv.at[at], x=dev)
 
     def xpass(who, at, piece, send, recv, dev):
         part = attg.at[who, at, pl.ds(piece * mid_row, mid_row)]
         return remote(part, part, send.at[at], recv.at[at], x=dev)
 
-    xto_right = lambda at: xring(att.at[at], x, at, x_r, y_l, xright)
-    xto_left = lambda at: xring(att.at[at], x, at, x_l, y_r, xleft)
-    xfrom_left = lambda at: xring(att.at[at], xleft, at, x_r, y_l, xleft)
-    xfrom_right = lambda at: xring(att.at[at], xright, at, x_l, y_r, xright)
+    xto_right = lambda at: xring(x, at, x_r, y_l, xright)
+    xto_left = lambda at: xring(x, at, x_l, y_r, xleft)
+    xfrom_left = lambda at: xring(xleft, at, x_r, y_l, xleft)
+    xfrom_right = lambda at: xring(xright, at, x_l, y_r, xright)
     xpass_right = lambda at: xpass(xleft, at, 0, x_fr, y_fl, xright)
     xpass_left = lambda at: xpass(xright, at, 1, x_fl, y_fr, xleft)
     xfar_left = lambda at: xpass(xfar, at, 0, x_fr, y_fl, xleft)
@@ -523,8 +520,7 @@
             jnp.concatenate([share, jnp.zeros_like(share)], axis=0), widen, (((0,), (0,)), ((), ())),
             preferred_element_type=F32, precision=lax.Precision.HIGHEST)
         value = os[at] + wide * (ro[at].astype(F32) - os[at])
-        att[at] = value.astype(BF16)
-        keep(at).start()
+        attg[x, at] = value.astype(BF16)
         xto_right(at).start()
         xto_left(at).start()
 
@@ -602,38 +598,70 @@
     each(Z, hz, settle_send)
     each(hz, 1, forward)
 
-    def late(i):
-        arrive(i)
-
-        @pl.when(i > Z // 2)
-        def _():
-            forward(i - 1)
-
-    each(Z, Z // 2, late)
-    forward(Z - 1)
-
-    def finish(at):
-        xfar_left(at).wait_recv()
-        xfar_right(at).wait_recv()
-        keep(at).wait()
-        for copy in (xto_right(at), xto_left(at), xpass_right(at), xpass_left(at), to_right(at), to_left(at)):
-            copy.wait_send()
-
-        @pl.when(at % 2 == 0)
-        def _():
-            pass_right(at).wait_send()
-
-        @pl.when(at % 2 == 1)
-        def _():
-            pass_left(at).wait_send()
-
-        for piece in range(Y):
-            to_twin(piece, at).wait_send()
-
-    each(Z, 0, finish)
     w_keep.wait()
     w_pass(xfar, 0, 4, 6, xleft).wait_recv()
     w_pass(xfar, 1, 5, 7, xright).wait_recv()
+    width = xv.shape[2]
+    row8 = lax.broadcasted_iota(jnp.int32, (8, slot), 0)
+
+    def collect(i):
+        at = home(i)
+        xfar_left(at).wait_recv()
+        xfar_right(at).wait_recv()
+        place = order[at]
+        rows = jnp.concatenate([attg[p, at] for p in range(X)], axis=1)
+        value = jnp.dot(rows, w_all[...].reshape(X * cols, width), preferred_element_type=F32)
+        ytmp[...] = value
+        yown[at] = ytmp[:, pl.ds(pl.multiple_of(x * cols, cols), cols)]
+        hidden = xv[place].astype(F32) + value
+        square = jnp.sum(hidden * hidden, axis=1, keepdims=True)
+        weighted = jnp.sum(hidden * (gain_ref[...] * read_ref[...]), axis=1, keepdims=True)
+        score = weighted * lax.rsqrt(square / width + 1e-06)
+        member = jnp.where((row8 < 2) & (segment(place) == row8), 1.0, 0.0)
+        sums = jnp.dot(member, jnp.broadcast_to(score, (slot, 128)),
+                       preferred_element_type=F32, precision=lax.Precision.HIGHEST)
+        means[at] = sums / jnp.maximum(jnp.sum(member, axis=1, keepdims=True), 1.0)
+
+    def late(i):
+        collect(i - hz)
+        arrive(i)
+
+        @pl.when(i > Z // 2)
+        def _():
+            forward(i - 1)
+
+    each(Z, hz, late)
+    forward(Z - 1)
+    each(Z, hz, collect)
+    outs = []
+    lane8 = lax.broadcasted_iota(jnp.int32, (8, 128), 1)
+    pooled = jnp.zeros((8, 128), F32)
+    for j in range(Z):
+        query = slot_query[j]
+        yout[j] = yown[query]
+        outs.append(pltpu.make_async_copy(yout.at[j], upd.at[j], out_sem.at[j]))
+        outs[j].start()
+        mean = means[query]
+        for k in range(2):
+            pooled = jnp.where(lane8 == 2 * j + k, jnp.broadcast_to(mean[k:k + 1], (8, 128)), pooled)
+    pool[...] = pooled
+
+    def finish(at):
+        for copy in (xto_right(at), xto_left(at), xpass_right(at), xpass_left(at), to_right(at), to_left(at)):
+            copy.wait_send()
+
+        @pl.when(at % 2 == 0)
+        def _():
+            pass_right(at).wait_send()
+
+        @pl.when(at % 2 == 1)
+        def _():
+            pass_left(at).wait_send()
+
+        for piece in range(Y):
+            to_twin(piece, at).wait_send()
+
+    each(Z, 0, finish)
     for copy in (w_whole(x, 0, 2, xright), w_whole(x, 1, 3, xleft),
                  w_pass(xleft, 0, 4, 6, xright), w_pass(xright, 1, 5, 7, xleft)):
         copy.wait_send()
@@ -651,29 +679,8 @@
         remote(cvar, va.at[to], s_va.at[to], r_va.at[to], y=to // C, c=to % C).wait_send()
 
     each(W, 1, end_cluster)
-
-
-def out_kernel(dq, ids, att_ref, next_ref, w_ref, x_ref, seg_ref, gain_ref, read_ref, upd_ref, pool_ref, y_ref):
-    step = pl.program_id(0)
-    parts, slot, cols = att_ref.shape[0], att_ref.shape[2], att_ref.shape[3]
-    rows = [jnp.concatenate([ref[p, 0] for p in range(parts)], axis=1) for ref in (att_ref, next_ref)]
-    y = jnp.dot(jnp.concatenate(rows, axis=0), w_ref[...], preferred_element_type=F32)
-    y_ref[...] = y
-    upd_ref[...] = y_ref[:, pl.ds(pl.multiple_of(ids[1] * cols, cols), cols)]
-    hidden = x_ref[...].astype(F32) + y
-    square = jnp.sum(hidden * hidden, axis=1, keepdims=True)
-    weighted = jnp.sum(hidden * (gain_ref[...] * read_ref[...]), axis=1, keepdims=True)
-    score = weighted * lax.rsqrt(square / y.shape[1] + 1e-06)
-    row = lax.broadcasted_iota(jnp.int32, (8, slot), 0)
-    for n in range(2):
-        first = (ids[0] * pl.num_programs(0) * 2 + step * 2 + n) * 2
-        member = jnp.where((row < 2) & (seg_ref[n] - first == row), 1.0, 0.0)
-        own = jnp.broadcast_to(score[n * slot:n * slot + slot], (slot, 128))
-        sums = jnp.dot(member, own, preferred_element_type=F32, precision=lax.Precision.HIGHEST)
-        count = jnp.maximum(jnp.sum(member, axis=1, keepdims=True), 1.0)
-        mean = sums / count
-        for k in range(2):
-            pool_ref[step * 4 + n * 2 + k] = mean[k, 0]
+    for copy in outs:
+        copy.wait()
 
 
 def body(sizes, doc_x, doc_seg, doc_query, doc_var, query_len, block_perm, cache_k, cache_v, cache_var,
@@ -704,16 +711,17 @@
     smem = pl.BlockSpec(memory_space=pltpu.SMEM)
     vmem = pl.BlockSpec(memory_space=pltpu.VMEM)
     hbm = pl.BlockSpec(memory_space=ANY)
-    attended, w_all, ids = pl.pallas_call(
+    update, pooled = pl.pallas_call(
         functools.partial(attention_kernel, sizes),
-        in_specs=[smem] * 4 + [vmem] * 5 + [hbm] * 8,
-        out_specs=[hbm] * 2 + [smem],
+        in_specs=[smem] * 4 + [vmem] * 5 + [hbm] * 4 + [vmem] * 2 + [hbm] * 4,
+        out_specs=[hbm, vmem],
         out_shape=[
-            jax.ShapeDtypeStruct((X, Z, slot, cols), BF16),
-            jax.ShapeDtypeStruct((X, cols, features), BF16),
-            jax.ShapeDtypeStruct((2,), i32),
+            jax.ShapeDtypeStruct((Z, slot, cols), F32),
+            jax.ShapeDtypeStruct((8, 128), F32),
         ],
         scratch_shapes=[
+            vm(X, Z, slot, cols), vm(X, cols, features), vf(slot, features), vf(Z, slot, cols), vf(Z, slot, cols),
+            vf(Z, 8, 128),
             pltpu.SMEM((blocks,), i32), vm(Z, slot, features), vm(features, cols), vm(features, cols), vm(features, cols),
             pltpu.SMEM((Z,), i32),
             vm(W, Z, piece, cols), vm(Z * W, piece, cols), vm(Z * bpq, piece, cols),
@@ -724,48 +732,20 @@
             vf(Z, slot, cols), vf(Z, 8, slot), vm(Y, part_keys, 128), vm(Z, slot, cols),
             vm(heads, Y, part_keys, 128), vm(heads, Y, part_keys, 128), vm(heads, tokens, 128),
             vf(heads, tokens, 128), vf(heads, tokens, 128),
-            vm(Z, slot, cols), vf(Z, 8, slot), vm(Z, slot, cols), vf(Z, 8, slot), vm(Z, slot, cols),
+            vm(Z, slot, cols), vf(Z, 8, slot), vm(Z, slot, cols), vf(Z, 8, slot),
             dma((4,)),
         ] + [dma((W,))] * 4 + [dma((Z,))] * 10 + [dma((Z,))] * 8 + [dma((Y, Z))] * 2
-        + [dma((Z,))] * 4 + [dma((Z,))] * 9 + [dma((5,)), dma((9,))],
+        + [dma((Z,))] * 4 + [dma((Z,))] * 8 + [dma((5,)), dma((9,)), dma((Z,))],
         compiler_params=pltpu.CompilerParams(
             collective_id=0, has_side_effects=True, vmem_limit_bytes=56 << 20),
         name="attention",
     )(block_perm, doc_query, query_len, var_bias, seg, doc_var.reshape(Z, 1, slot),
       jnp.asarray(np.cos(turns), F32), jnp.asarray(np.sin(turns), F32), jnp.asarray(frequency)[None, :],
       doc_x.reshape(Z, slot, features), w_query, w_key, w_value,
+      norm_gain.reshape(1, features), readout.reshape(1, features),
       cache_k.reshape(Y, Z, piece, cols), cache_v.reshape(Y, Z, piece, cols), cache_var.reshape(Y, 1, slot), w_out)
 
-    full = lambda *shape: pl.BlockSpec(shape, lambda i, *_: (0,) * len(shape))
-    update, pooled = pl.pallas_call(
-        out_kernel,
-        grid_spec=pltpu.PrefetchScalarGridSpec(
-            num_scalar_prefetch=2,
-            grid=(Z // 2,),
-            in_specs=[
-                pl.BlockSpec((X, 1, slot, cols), lambda i, d, n: (0, d[n[0] * 2 * Z + 4 * i], 0, 0)),
-                pl.BlockSpec((X, 1, slot, cols), lambda i, d, n: (0, d[n[0] * 2 * Z + 4 * i + 2], 0, 0)),
-                full(X * cols, features),
-                pl.BlockSpec((2 * slot, features), lambda i, d, n: (i, 0)),
-                pl.BlockSpec((2, 1, slot), lambda i, d, n: (i, 0, 0)),
-                full(1, features),
-                full(1, features),
-            ],
-            out_specs=[
-                pl.BlockSpec((2 * slot, cols), lambda i, d, n: (i, 0)),
-                smem,
-            ],
-            scratch_shapes=[pltpu.VMEM((2 * slot, features), F32)],
-        ),
-        out_shape=[
-            jax.ShapeDtypeStruct((tokens, cols), F32),
-            jax.ShapeDtypeStruct((2 * Z,), F32),
-        ],
-        compiler_params=pltpu.CompilerParams(vmem_limit_bytes=60 << 20),
-        name="out_part",
-    )(doc_query, ids, attended, attended, w_all.reshape(X * cols, features), doc_x, seg, norm_gain.reshape(1, features),
-      readout.reshape(1, features))
-    return update, pooled
+    return update.reshape(tokens, cols), pooled[0, :2 * Z]
 
 
 def solution(mesh):

time: 127 us -> 124 us (0.976)
  Pallas kernels: 125 us -> 119 us
  local copies, waits for them, and re-layouts: 0 us -> 3.45 us
    pallas_call x1 -> x0, Pallas kernels: 8.03 us -> none  [body(): pl.pallas_call(out_kernel, grid_spec=pltpu.PrefetchScalarGridSpec(num_sca...]
    unnamed x0 -> x1, local copies, waits for them, and re-layouts: none -> 2.26 us
    pallas_call x1, Pallas kernels: 117 us -> 119 us  [body(): pl.pallas_call(functools.partial(attention_kernel, sizes), in_specs=[smem...]
where the time goes in v7:
time: 124 us; the launch traced here: 123 us
  Pallas kernels  119 us (96%)
  local copies, waits for them, and re-layouts  3.45 us (3%)
    pallas_call x1, Pallas kernels, body(): pl.pallas_call(functools.partial(attention_kernel, sizes), in_specs=[smem...  119 us

profile of v7, /device:TPU:8, one launch (start us, length us, event | category | flops | bytes accessed | tf_op | source)
XLA Modules:
  0.0 123.0 jit_solution(6240969584434640261)
XLA Ops:
  0.6 118.9 %attention.1 = (f32[8,128,256]{2,1,0:T(8,128)}, f32[8,128]{1,0:T(8,128)}) custom-call(s32[64]{0:T(128)} %perm.1, s32[1024]{0:T(1024)} %dq.1, s32[8]{0:T(128)} %qlen.1, f32[2,4]{1,0:T(2,128)} %bias.1, s32[8,1,128]{2,1,0:T(1,128)} %bitcast.15, s32[8,1,128]{2,1,0:T(1,128)} %bitcast.16, f32[128,128]{1,0:T(8,128)} %constant.6.clone.tcos_ref, ...), custom_call_target="tpu_custom_call" | custom-call | tf_op jit(solution)/shard_map/attention/pallas_call | solution.py:714
  119.6 1.2 slice_bitcast_fusion
  120.8 2.3 %copy.22 = f32[1024,256]{1,0:T(8,128)} copy(f32[1024,256]{1,0:T(8,128)} %bitcast.12) | data formatting | bytes 2097152

commit v8 on v7

--- a/solution.py
+++ b/solution.py
@@ -40,8 +40,8 @@
 
 
 def attention_kernel(
-    sizes, perm, dq, qlen, bias, seg_ref, var_ref, tcos_ref, tsin_ref, freq_ref, x_in, wq_in, wk_in, wv_in, gain_ref, read_ref, ck, cv, cvar, w_in, upd, pool,
-    attg, w_all, ytmp, yown, yout, means, inv, xv, wq, wk, wv, order, abuf, bbuf, gbuf, va, vb, kv, qrot, qh, dv, hv, cosv, sinv, qtab, ktab,
+    sizes, perm, dq, qlen, bias, seg_ref, var_ref, tcos_ref, tsin_ref, freq_ref, x_in, wq_in, wk_in, wv_in, gain_ref, read_ref, ck, cv, cvar, w_in, upd, means,
+    attg, w_all, ytmp, yown, inv, xv, wq, wk, wv, order, abuf, bbuf, gbuf, va, vb, kv, qrot, qh, dv, hv, cosv, sinv, qtab, ktab,
     os, sts, kfs, qfs, ka, vx, qa, acc, mx, oh, sth, ro, rst,
     s_x, s_a, r_a, s_va, r_va, s_b, r_b, s_vb, r_vb, s_g, r_g, s_q, r_q, s_dv, r_dv,
     s_r, s_l, r_l, r_r, s_fr, s_fl, r_fl, r_fr, s_s, r_s,
@@ -604,6 +604,8 @@
     width = xv.shape[2]
     row8 = lax.broadcasted_iota(jnp.int32, (8, slot), 0)
 
+    give = lambda at: pltpu.make_async_copy(yown.at[at], upd.at[at], out_sem.at[at])
+
     def collect(i):
         at = home(i)
         xfar_left(at).wait_recv()
@@ -613,6 +615,7 @@
         value = jnp.dot(rows, w_all[...].reshape(X * cols, width), preferred_element_type=F32)
         ytmp[...] = value
         yown[at] = ytmp[:, pl.ds(pl.multiple_of(x * cols, cols), cols)]
+        give(at).start()
         hidden = xv[place].astype(F32) + value
         square = jnp.sum(hidden * hidden, axis=1, keepdims=True)
         weighted = jnp.sum(hidden * (gain_ref[...] * read_ref[...]), axis=1, keepdims=True)
@@ -633,18 +636,6 @@
     each(Z, hz, late)
     forward(Z - 1)
     each(Z, hz, collect)
-    outs = []
-    lane8 = lax.broadcasted_iota(jnp.int32, (8, 128), 1)
-    pooled = jnp.zeros((8, 128), F32)
-    for j in range(Z):
-        query = slot_query[j]
-        yout[j] = yown[query]
-        outs.append(pltpu.make_async_copy(yout.at[j], upd.at[j], out_sem.at[j]))
-        outs[j].start()
-        mean = means[query]
-        for k in range(2):
-            pooled = jnp.where(lane8 == 2 * j + k, jnp.broadcast_to(mean[k:k + 1], (8, 128)), pooled)
-    pool[...] = pooled
 
     def finish(at):
         for copy in (xto_right(at), xto_left(at), xpass_right(at), xpass_left(at), to_right(at), to_left(at)):
@@ -679,7 +670,22 @@
         remote(cvar, va.at[to], s_va.at[to], r_va.at[to], y=to // C, c=to % C).wait_send()
 
     each(W, 1, end_cluster)
-    for copy in outs:
+    each(Z, 0, lambda at: give(at).wait())
+
+
+def order_kernel(sizes, dq, by_query, means, upd, pool, sem):
+    X, Y, Z, C = sizes
+    blk = (lax.axis_index("y") * Z + lax.axis_index("z")) * C + lax.axis_index("c")
+    copies = []
+    for j in range(Z):
+        query = dq[blk * 2 * Z + 2 * j]
+        copies.append(pltpu.make_async_copy(by_query.at[query], upd.at[j], sem.at[j]))
+        copies[j].start()
+    for j in range(Z):
+        mean = means[dq[blk * 2 * Z + 2 * j]]
+        for k in range(2):
+            pool[2 * j + k] = mean[k, 0]
+    for copy in copies:
         copy.wait()
 
 
@@ -711,17 +717,16 @@
     smem = pl.BlockSpec(memory_space=pltpu.SMEM)
     vmem = pl.BlockSpec(memory_space=pltpu.VMEM)
     hbm = pl.BlockSpec(memory_space=ANY)
-    update, pooled = pl.pallas_call(
+    by_query, means = pl.pallas_call(
         functools.partial(attention_kernel, sizes),
         in_specs=[smem] * 4 + [vmem] * 5 + [hbm] * 4 + [vmem] * 2 + [hbm] * 4,
         out_specs=[hbm, vmem],
         out_shape=[
             jax.ShapeDtypeStruct((Z, slot, cols), F32),
-            jax.ShapeDtypeStruct((8, 128), F32),
+            jax.ShapeDtypeStruct((Z, 8, 128), F32),
         ],
         scratch_shapes=[
-            vm(X, Z, slot, cols), vm(X, cols, features), vf(slot, features), vf(Z, slot, cols), vf(Z, slot, cols),
-            vf(Z, 8, 128),
+            vm(X, Z, slot, cols), vm(X, cols, features), vf(slot, features), vf(Z, slot, cols),
             pltpu.SMEM((blocks,), i32), vm(Z, slot, features), vm(features, cols), vm(features, cols), vm(features, cols),
             pltpu.SMEM((Z,), i32),
             vm(W, Z, piece, cols), vm(Z * W, piece, cols), vm(Z * bpq, piece, cols),
@@ -745,7 +750,19 @@
       norm_gain.reshape(1, features), readout.reshape(1, features),
       cache_k.reshape(Y, Z, piece, cols), cache_v.reshape(Y, Z, piece, cols), cache_var.reshape(Y, 1, slot), w_out)
 
-    return update.reshape(tokens, cols), pooled[0, :2 * Z]
+    update, pooled = pl.pallas_call(
+        functools.partial(order_kernel, sizes),
+        in_specs=[smem, hbm, vmem],
+        out_specs=[hbm, smem],
+        out_shape=[
+            jax.ShapeDtypeStruct((Z, slot, cols), F32),
+            jax.ShapeDtypeStruct((2 * Z,), F32),
+        ],
+        scratch_shapes=[dma((Z,))],
+        compiler_params=pltpu.CompilerParams(vmem_limit_bytes=60 << 20),
+        name="slot_order",
+    )(doc_query, by_query, means)
+    return update.reshape(tokens, cols), pooled
 
 
 def solution(mesh):

time: 124 us -> 154 us (1.24)
  Pallas kernels: 119 us -> 153 us
  local copies, waits for them, and re-layouts: 3.45 us -> 0 us
    pallas_call x0 -> x1, Pallas kernels: none -> 34.2 us  [body(): pl.pallas_call(functools.partial(order_kernel, sizes), in_specs=[smem, hb...]
    unnamed x1 -> x0, local copies, waits for them, and re-layouts: 2.26 us -> none
where the time goes in v8:
time: 154 us; the launch traced here: 153 us
  Pallas kernels  153 us (99%)
    pallas_call x1, Pallas kernels, body(): pl.pallas_call(functools.partial(attention_kernel, sizes), in_specs=[smem...  119 us
    pallas_call x1, Pallas kernels, body(): pl.pallas_call(functools.partial(order_kernel, sizes), in_specs=[smem, hb...  34.2 us

profile of v8, /device:TPU:8, one launch (start us, length us, event | category | flops | bytes accessed | tf_op | source)
XLA Modules:
  0.0 153.4 jit_solution(12558406677629727080)
XLA Ops:
  0.6 118.5 %attention.1 = (f32[8,128,256]{2,1,0:T(8,128)}, f32[8,8,128]{2,1,0:T(8,128)}) custom-call(s32[64]{0:T(128)} %perm.1, s32[1024]{0:T(1024)} %dq.3, s32[8]{0:T(128)} %qlen.1, f32[2,4]{1,0:T(2,128)} %bias.1, s32[8,1,128]{2,1,0:T(1,128)} %bitcast.12, s32[8,1,128]{2,1,0:T(1,128)} %bitcast.13, f32[128,128]{1,0:T(8,128)} %constant.6.clone.tcos_ref, ...), custom_call_target="tpu_custom_call" | custom-call | tf_op jit(solution)/shard_map/attention/pallas_call | solution.py:720
  119.2 34.2 %slot_order.1 = (f32[8,128,256]{2,1,0:T(8,128)}, f32[16]{0:T(128)}) custom-call(s32[1024]{0:T(1024)} %dq.3, f32[8,128,256]{2,1,0:T(8,128)} %get-tuple-element.6.by_query, f32[8,8,128]{2,1,0:T(8,128)} %get-tuple-element.7.means), custom_call_target="tpu_custom_call" | custom-call | tf_op jit(solution)/shard_map/slot_order/pallas_call | solution.py:753

commit v9 on v8

--- a/solution.py
+++ b/solution.py
@@ -673,13 +673,14 @@
     each(Z, 0, lambda at: give(at).wait())
 
 
-def order_kernel(sizes, dq, by_query, means, upd, pool, sem):
+def order_kernel(sizes, dq, by_query, means, upd, pool, staged, sem):
     X, Y, Z, C = sizes
     blk = (lax.axis_index("y") * Z + lax.axis_index("z")) * C + lax.axis_index("c")
     copies = []
     for j in range(Z):
         query = dq[blk * 2 * Z + 2 * j]
-        copies.append(pltpu.make_async_copy(by_query.at[query], upd.at[j], sem.at[j]))
+        staged[j] = by_query[query]
+        copies.append(pltpu.make_async_copy(staged.at[j], upd.at[j], sem.at[j]))
         copies[j].start()
     for j in range(Z):
         mean = means[dq[blk * 2 * Z + 2 * j]]
@@ -752,13 +753,13 @@
 
     update, pooled = pl.pallas_call(
         functools.partial(order_kernel, sizes),
-        in_specs=[smem, hbm, vmem],
+        in_specs=[smem, vmem, vmem],
         out_specs=[hbm, smem],
         out_shape=[
             jax.ShapeDtypeStruct((Z, slot, cols), F32),
             jax.ShapeDtypeStruct((2 * Z,), F32),
         ],
-        scratch_shapes=[dma((Z,))],
+        scratch_shapes=[vf(Z, slot, cols), dma((Z,))],
         compiler_params=pltpu.CompilerParams(vmem_limit_bytes=60 << 20),
         name="slot_order",
     )(doc_query, by_query, means)

time: 154 us -> 123 us (0.80)
  Pallas kernels: 153 us -> 121 us
    pallas_call x1, Pallas kernels: 34.2 us -> 2.81 us  [body(): pl.pallas_call(functools.partial(order_kernel, sizes), in_specs=[smem, vm...]
where the time goes in v9:
time: 123 us; the launch traced here: 122 us
  Pallas kernels  121 us (98%)
    pallas_call x1, Pallas kernels, body(): pl.pallas_call(functools.partial(attention_kernel, sizes), in_specs=[smem...  118 us
    pallas_call x1, Pallas kernels, body(): pl.pallas_call(functools.partial(order_kernel, sizes), in_specs=[smem, vm...  2.81 us

profile of v9, /device:TPU:8, one launch (start us, length us, event | category | flops | bytes accessed | tf_op | source)
XLA Modules:
  0.0 121.9 jit_solution(980455821244642495)
XLA Ops:
  0.6 118.5 %attention.1 = (f32[8,128,256]{2,1,0:T(8,128)}, f32[8,8,128]{2,1,0:T(8,128)}) custom-call(s32[64]{0:T(128)} %perm.1, s32[1024]{0:T(1024)} %dq.3, s32[8]{0:T(128)} %qlen.1, f32[2,4]{1,0:T(2,128)} %bias.1, s32[8,1,128]{2,1,0:T(1,128)} %bitcast.12, s32[8,1,128]{2,1,0:T(1,128)} %bitcast.13, f32[128,128]{1,0:T(8,128)} %constant.6.clone.tcos_ref, ...), custom_call_target="tpu_custom_call" | custom-call | tf_op jit(solution)/shard_map/attention/pallas_call | solution.py:721
  119.1 2.8 %slot_order.1 = (f32[8,128,256]{2,1,0:T(8,128)}, f32[16]{0:T(128)}) custom-call(s32[1024]{0:T(1024)} %dq.3, f32[8,128,256]{2,1,0:T(8,128)} %get-tuple-element.6.by_query, f32[8,8,128]{2,1,0:T(8,128)} %get-tuple-element.7.means), custom_call_target="tpu_custom_call" | custom-call | tf_op jit(solution)/shard_map/slot_order/pallas_call | solution.py:754
